TPU v7x, 32 devices: a whole 2x2x4 slice. The times are simulated.
32 devices in a mesh: fsdp: 2 (over x), ctx: 4 (over z), tp: 4 (over y, core).
Axes of the slice: x: 2, y: 2, z: 4, core: 2. Of those that a mesh axis runs over, the one named last changes fastest.
Arguments:
- inputs: bfloat16 [2, 1024, 2048], P('fsdp', 'ctx'), may hold values from -6 to 6
- attn_gain: bfloat16 [2048], P(('fsdp', 'ctx')), may hold values from 0.099609375 to 1.8984375
- qkv_weight: bfloat16 [2048, 3, 2048], P(('fsdp', 'ctx'), None, 'tp'), may hold values from -0.125 to 0.125
- out_weight: bfloat16 [2048, 2048], P(('fsdp', 'ctx'), 'tp'), may hold values from -1 to 1
- qk_gains: bfloat16 [2, 2048], P(None, 'tp'), may hold values from 0.099609375 to 1.8984375
- mlp_gain: bfloat16 [2048], P(('fsdp', 'ctx')), may hold values from 0.099609375 to 1.8984375
- router_weight: bfloat16 [2048, 8], P(('fsdp', 'ctx')), may hold values from -0.0625 to 0.0625
- gate_up_weight: bfloat16 [2048, 2, 8, 1024], P(('fsdp', 'ctx'), None, None, 'tp'), may hold values from -0.125 to 0.125
- down_weight: bfloat16 [2048, 8, 1024], P(('fsdp', 'ctx'), None, 'tp'), may hold values from -1.5 to 1.5
- routes: int32 [4, 2, 256, 4], P('ctx', 'fsdp'), may hold values from 0 to 7, all different within a row; in each aligned block of 256 rows (0 to 255, 256 to 511, ..., all dimensions but the last counted through in order) at most 160 rows name the same one
- cotangent: bfloat16 [2, 1024, 2048], P('fsdp', 'ctx'), may hold values from -6 to 6
Outputs:
- output: bfloat16 [2, 1024, 2048], P('fsdp', 'ctx')
- grad_inputs: float32 [2, 1024, 2048], P('fsdp', 'ctx')
- grad_attn_gain: float32 [2048], P(('fsdp', 'ctx'))
- grad_qkv: float32 [2048, 3, 2048], P(('fsdp', 'ctx'), None, 'tp')
- grad_out: float32 [2048, 2048], P(('fsdp', 'ctx'), 'tp')
- grad_qk_gains: float32 [2, 2048], P(None, 'tp')
- grad_mlp_gain: float32 [2048], P(('fsdp', 'ctx'))
- grad_router: float32 [2048, 8], P(('fsdp', 'ctx'))
- grad_gate_up: float32 [2048, 2, 8, 1024], P(('fsdp', 'ctx'), None, None, 'tp')
- grad_down: float32 [2048, 8, 1024], P(('fsdp', 'ctx'), None, 'tp')
Inputs may be any that keep to these rules, and one draw needn't show every extreme that they name: `routes`: each row names 4 different experts. Among the 256 tokens of one device (aligned blocks of the array in its order) no expert is named more than 160 times, a bound that some block reaches.
All inputs are finite; a program needn't handle non-finite values.
Results may differ from a plain program's by a relative error of at most 0.017.
Values may be sent and summed in bfloat16 or wider, within the bound.
A program may use at most 256 MiB of HBM per device.

v0:
```python
import math

import jax
import jax.numpy as jnp
from jax import lax
from jax.sharding import PartitionSpec as P

HEAD_DIM = 128
TOPK = 4
EXPERTS = 8
HQ = 2048
CAP = 160


epsilon = 1e-05
highest = lax.Precision.HIGHEST


def inv_rms(values):
    return lax.rsqrt(jnp.mean(values * values, axis=-1, keepdims=True) + epsilon)


def rotary_tables(offset, length):
    half_dim = HEAD_DIM // 2
    frequency = jnp.exp(
        jnp.arange(half_dim, dtype=jnp.float32) * (-2.0 * math.log(10000.0) / HEAD_DIM)
    )
    positions = (offset + jnp.arange(length, dtype=jnp.int32)).astype(jnp.float32)
    angles = positions[:, None] * frequency[None, :]
    angles = jnp.concatenate([angles, angles], axis=1)
    return (jnp.cos(angles), jnp.sin(angles))


def rotate(values, cosine, sine_table):
    half_dim = values.shape[-1] // 2
    turned = jnp.concatenate([-values[..., half_dim:], values[..., :half_dim]], axis=-1)
    return values * cosine + turned * sine_table


def rotate_back(grads, cosine, sine_table):
    half_dim = grads.shape[-1] // 2
    scaled = grads * sine_table
    return grads * cosine + jnp.concatenate(
        [scaled[..., half_dim:], -scaled[..., :half_dim]], axis=-1
    )


def slot_table(routed):
    flat_routes = routed.reshape(-1)
    one_hot = (flat_routes[:, None] == jnp.arange(EXPERTS, dtype=jnp.int32)[None, :]).astype(
        jnp.int32
    )
    earlier = jnp.cumsum(one_hot, axis=0) - one_hot
    within = jnp.sum(earlier * one_hot, axis=1)
    slots = flat_routes * CAP + within
    owners = jnp.arange(flat_routes.shape[0], dtype=jnp.int32) // TOPK
    token_of = jnp.zeros((EXPERTS * CAP,), jnp.int32).at[slots].set(owners)
    filled = jnp.zeros((EXPERTS * CAP,), jnp.float32).at[slots].set(1.0)
    return (slots.reshape(routed.shape), token_of, filled)


def on_device(
    inputs,
    attn_gain,
    qkv_weight,
    out_weight,
    qk_gains,
    mlp_gain,
    router_weight,
    gate_up_weight,
    down_weight,
    routes,
    cotangent,
):
    seq_dev, block, width = inputs.shape
    rows = seq_dev * block
    heads_dev = qkv_weight.shape[2] // HEAD_DIM
    scale = 1.0 / math.sqrt(HEAD_DIM)
    place = lax.axis_index("ctx")
    attn_gain_all, qkv_all, out_all, mlp_gain_all, router_all = (
        lax.all_gather(attn_gain, ("fsdp", "ctx"), axis=0, tiled=True),
        lax.all_gather(qkv_weight, ("fsdp", "ctx"), axis=0, tiled=True),
        lax.all_gather(out_weight, ("fsdp", "ctx"), axis=0, tiled=True),
        lax.all_gather(mlp_gain, ("fsdp", "ctx"), axis=0, tiled=True),
        lax.all_gather(router_weight, ("fsdp", "ctx"), axis=0, tiled=True),
    )
    attn_scale = attn_gain_all.astype(jnp.float32)
    mlp_scale = mlp_gain_all.astype(jnp.float32)
    flat_in = inputs.reshape(rows, width).astype(jnp.float32)
    first_rms = inv_rms(flat_in)
    normed = (flat_in * first_rms * attn_scale).astype(jnp.bfloat16)
    projected = jnp.einsum("td,dch->tch", normed, qkv_all, preferred_element_type=jnp.float32)
    query_proj = projected[:, 0]
    key_proj = projected[:, 1]
    query_sums, key_sums = lax.psum(
        (jnp.sum(query_proj * query_proj, axis=-1), jnp.sum(key_proj * key_proj, axis=-1)), "tp"
    )
    query_rms = lax.rsqrt(query_sums / HQ + epsilon)[:, None]
    key_rms = lax.rsqrt(key_sums / HQ + epsilon)[:, None]
    query_gain = qk_gains[0].astype(jnp.float32)
    key_gain = qk_gains[1].astype(jnp.float32)
    query_norm = query_proj * query_rms * query_gain
    key_norm = key_proj * key_rms * key_gain
    cosine, sine_table = rotary_tables(place * block, block)
    cos_heads = cosine[:, None, :]
    sin_heads = sine_table[:, None, :]
    head_shape = (seq_dev, block, heads_dev, HEAD_DIM)
    query_rot = rotate(query_norm.reshape(head_shape), cos_heads, sin_heads).astype(jnp.bfloat16)
    key_rot = rotate(key_norm.reshape(head_shape), cos_heads, sin_heads).astype(jnp.bfloat16)
    value_heads = projected[:, 2].reshape(head_shape).astype(jnp.bfloat16)
    key_all, value_all = (
        lax.all_gather(key_rot, "ctx", axis=1, tiled=True),
        lax.all_gather(value_heads, "ctx", axis=1, tiled=True),
    )
    length = key_all.shape[1]
    key_block = jnp.arange(length, dtype=jnp.int32) // block
    allowed = (key_block <= place)[None, None, None, :]
    scores = (
        jnp.einsum("sqhd,skhd->shqk", query_rot, key_all, preferred_element_type=jnp.float32)
        * scale
    )
    scores = jnp.where(allowed, scores, -1e30)
    top_score = jnp.max(scores, axis=-1, keepdims=True)
    exponent = jnp.exp(scores - top_score)
    total = jnp.sum(exponent, axis=-1, keepdims=True)
    log_total = top_score + jnp.log(total)
    softmaxed = exponent / total
    attended = jnp.einsum(
        "shqk,skhd->sqhd",
        softmaxed.astype(jnp.bfloat16),
        value_all,
        preferred_element_type=jnp.float32,
    )
    attended = attended.reshape(rows, heads_dev * HEAD_DIM).astype(jnp.bfloat16)
    branch = lax.psum(
        jnp.einsum("th,dh->td", attended, out_all, preferred_element_type=jnp.float32), "tp"
    )
    middle = flat_in + branch
    second_rms = inv_rms(middle)
    normed_mlp = (middle * second_rms * mlp_scale).astype(jnp.bfloat16)
    logits = jnp.dot(normed_mlp, router_all, preferred_element_type=jnp.float32)
    chances = jax.nn.softmax(logits, axis=-1)
    routed = routes.reshape(rows, TOPK)
    gates = jnp.take_along_axis(chances, routed, axis=-1)
    slots, token_of, filled = slot_table(routed)
    dispatched = (normed_mlp[token_of] * filled[:, None].astype(jnp.bfloat16)).reshape(
        EXPERTS, CAP, width
    )
    gate_up_all, down_all = (
        lax.all_gather(gate_up_weight, ("fsdp", "ctx"), axis=0, tiled=True),
        lax.all_gather(down_weight, ("fsdp", "ctx"), axis=0, tiled=True),
    )
    gate_up = jnp.einsum(
        "ecd,djef->ecjf", dispatched, gate_up_all, preferred_element_type=jnp.float32
    )
    gate_part = gate_up[:, :, 0]
    up_part = gate_up[:, :, 1]
    activated = (jax.nn.silu(gate_part) * up_part).astype(jnp.bfloat16)
    upstream = cotangent.reshape(rows, width).astype(jnp.float32)
    slot_gates = (
        jnp.zeros((EXPERTS * CAP,), jnp.float32)
        .at[slots.reshape(-1)]
        .set(gates.reshape(-1))
        .reshape(EXPERTS, CAP)
    )
    token_grid = token_of.reshape(EXPERTS, CAP)
    filled_grid = filled.reshape(EXPERTS, CAP)

    def expert_forward(expert_index, running):
        combined, slot_products = running
        expert_down = lax.dynamic_index_in_dim(down_all, expert_index, 1, keepdims=False)
        expert_act = lax.dynamic_index_in_dim(activated, expert_index, 0, keepdims=False)
        expert_tokens = lax.dynamic_index_in_dim(token_grid, expert_index, 0, keepdims=False)
        expert_gates = lax.dynamic_index_in_dim(slot_gates, expert_index, 0, keepdims=False)
        returned_rows = jnp.einsum(
            "cf,df->cd", expert_act, expert_down, preferred_element_type=jnp.float32
        )
        combined = combined.at[expert_tokens].add(returned_rows * expert_gates[:, None])
        products = jnp.sum(returned_rows * upstream[expert_tokens], axis=-1)
        slot_products = lax.dynamic_update_index_in_dim(slot_products, products, expert_index, 0)
        return (combined, slot_products)

    combined, slot_products = lax.fori_loop(
        0,
        EXPERTS,
        expert_forward,
        (jnp.zeros((rows, width), jnp.float32), jnp.zeros((EXPERTS, CAP), jnp.float32)),
    )
    gate_grad_part = slot_products.reshape(-1)[slots]
    expert_sum = lax.psum(combined, "tp")
    output = (middle + expert_sum).astype(jnp.bfloat16).reshape(seq_dev, block, width)
    slot_grads = (
        (slot_gates.reshape(-1)[:, None] * upstream[token_of])
        .astype(jnp.bfloat16)
        .reshape(EXPERTS, CAP, width)
    )
    gate_up_back, down_back = (
        lax.all_gather(gate_up_weight, ("fsdp", "ctx"), axis=0, tiled=True),
        lax.all_gather(down_weight, ("fsdp", "ctx"), axis=0, tiled=True),
    )
    act_grads = jnp.einsum(
        "ecd,def->ecf", slot_grads, down_back, preferred_element_type=jnp.float32
    )
    sigmoid = jax.nn.sigmoid(gate_part)
    gate_grads = act_grads * up_part * sigmoid * (1.0 + gate_part * (1.0 - sigmoid))
    up_grads = act_grads * (gate_part * sigmoid)
    pre_grads = jnp.stack([gate_grads, up_grads], axis=2).astype(jnp.bfloat16)

    def expert_backward(expert_index, running):
        expert_pre = lax.dynamic_index_in_dim(pre_grads, expert_index, 0, keepdims=False)
        expert_weight = lax.dynamic_index_in_dim(gate_up_back, expert_index, 2, keepdims=False)
        expert_tokens = lax.dynamic_index_in_dim(token_grid, expert_index, 0, keepdims=False)
        expert_filled = lax.dynamic_index_in_dim(filled_grid, expert_index, 0, keepdims=False)
        expert_back = jnp.einsum(
            "cjf,djf->cd", expert_pre, expert_weight, preferred_element_type=jnp.float32
        )
        return running.at[expert_tokens].add(expert_back * expert_filled[:, None])

    expert_input_part = lax.fori_loop(
        0, EXPERTS, expert_backward, jnp.zeros((rows, width), jnp.float32)
    )
    gate_up_term = jnp.einsum(
        "ecd,ecjf->djef", dispatched, pre_grads, preferred_element_type=jnp.float32
    )
    down_term = jnp.einsum(
        "ecf,ecd->def", activated, slot_grads, preferred_element_type=jnp.float32
    )
    expert_grads = lax.psum_scatter(
        jnp.concatenate([gate_up_term, down_term[:, None]], axis=1),
        ("fsdp", "ctx"),
        scatter_dimension=0,
        tiled=True,
    )
    gate_up_share = expert_grads[:, :2]
    down_share = expert_grads[:, 2]
    expert_input, gate_total = lax.psum((expert_input_part, gate_grad_part), "tp")
    chosen = (routed[:, :, None] == jnp.arange(EXPERTS, dtype=jnp.int32)[None, None, :]).astype(
        jnp.float32
    )
    chance_grads = jnp.sum(gate_total[:, :, None] * chosen, axis=1)
    logit_grads = chances * (chance_grads - jnp.sum(chances * chance_grads, axis=-1, keepdims=True))
    router_f32 = router_all.astype(jnp.float32)
    mlp_input = expert_input + jnp.dot(logit_grads, router_f32.T, precision=highest)
    grad_router = jnp.dot(normed_mlp.astype(jnp.float32).T, logit_grads, precision=highest)
    grad_mlp_gain = jnp.sum(mlp_input * middle * second_rms, axis=0)
    scaled_mlp = mlp_input * mlp_scale
    middle_grad = (
        upstream
        + second_rms * scaled_mlp
        - middle * second_rms**3 / width * jnp.sum(scaled_mlp * middle, axis=-1, keepdims=True)
    )
    branch_grad = middle_grad.astype(jnp.bfloat16)
    grad_out = jnp.einsum("td,th->dh", branch_grad, attended, preferred_element_type=jnp.float32)
    attended_grad = (
        jnp.dot(branch_grad, out_all, preferred_element_type=jnp.float32)
        .astype(jnp.bfloat16)
        .reshape(head_shape)
    )
    again_scores = (
        jnp.einsum("sqhd,skhd->shqk", query_rot, key_all, preferred_element_type=jnp.float32)
        * scale
    )
    again_scores = jnp.where(allowed, again_scores, -1e30)
    recomputed = jnp.exp(again_scores - log_total)
    prob_grads = jnp.einsum(
        "sqhd,skhd->shqk", attended_grad, value_all, preferred_element_type=jnp.float32
    )
    score_grads = (
        recomputed * (prob_grads - jnp.sum(recomputed * prob_grads, axis=-1, keepdims=True))
    ).astype(jnp.bfloat16)
    query_grads = (
        jnp.einsum("shqk,skhd->sqhd", score_grads, key_all, preferred_element_type=jnp.float32)
        * scale
    )
    key_grads = (
        jnp.einsum("shqk,sqhd->skhd", score_grads, query_rot, preferred_element_type=jnp.float32)
        * scale
    )
    value_grads = jnp.einsum(
        "shqk,sqhd->skhd",
        recomputed.astype(jnp.bfloat16),
        attended_grad,
        preferred_element_type=jnp.float32,
    )
    key_back, value_back = (
        lax.psum_scatter(key_grads, "ctx", scatter_dimension=1, tiled=True),
        lax.psum_scatter(value_grads, "ctx", scatter_dimension=1, tiled=True),
    )
    query_norm_grad = rotate_back(query_grads, cos_heads, sin_heads).reshape(rows, -1)
    key_norm_grad = rotate_back(key_back, cos_heads, sin_heads).reshape(rows, -1)
    query_scaled = query_norm_grad * query_gain
    key_scaled = key_norm_grad * key_gain
    query_inner, key_inner = lax.psum(
        (jnp.sum(query_scaled * query_proj, axis=-1), jnp.sum(key_scaled * key_proj, axis=-1)), "tp"
    )
    query_pre = query_rms * query_scaled - query_proj * query_rms**3 / HQ * query_inner[:, None]
    key_pre = key_rms * key_scaled - key_proj * key_rms**3 / HQ * key_inner[:, None]
    gain_terms = jnp.stack(
        [
            jnp.sum(query_norm_grad * query_proj * query_rms, axis=0),
            jnp.sum(key_norm_grad * key_proj * key_rms, axis=0),
        ]
    )
    grad_qk_gains = lax.psum(gain_terms, ("fsdp", "ctx"))
    proj_grads = jnp.stack([query_pre, key_pre, value_back.reshape(rows, -1)], axis=1).astype(
        jnp.bfloat16
    )
    grad_qkv = jnp.einsum("td,tch->dch", normed, proj_grads, preferred_element_type=jnp.float32)
    normed_grad = lax.psum(
        jnp.einsum("tch,dch->td", proj_grads, qkv_all, preferred_element_type=jnp.float32), "tp"
    )
    grad_attn_gain = jnp.sum(normed_grad * flat_in * first_rms, axis=0)
    scaled_first = normed_grad * attn_scale
    grad_inputs = (
        middle_grad
        + first_rms * scaled_first
        - flat_in * first_rms**3 / width * jnp.sum(scaled_first * flat_in, axis=-1, keepdims=True)
    )
    shares = (
        lax.psum_scatter(grad_attn_gain, ("fsdp", "ctx"), scatter_dimension=0, tiled=True),
        lax.psum_scatter(grad_qkv, ("fsdp", "ctx"), scatter_dimension=0, tiled=True),
        lax.psum_scatter(grad_out, ("fsdp", "ctx"), scatter_dimension=0, tiled=True),
        lax.psum_scatter(grad_mlp_gain, ("fsdp", "ctx"), scatter_dimension=0, tiled=True),
        lax.psum_scatter(grad_router, ("fsdp", "ctx"), scatter_dimension=0, tiled=True),
    )
    return (
        output,
        grad_inputs.reshape(seq_dev, block, width),
        shares[0],
        shares[1],
        shares[2],
        grad_qk_gains,
        shares[3],
        shares[4],
        gate_up_share,
        down_share,
    )


def solution(mesh):
    placed = (
        P("fsdp", "ctx", None),
        P(("fsdp", "ctx")),
        P(("fsdp", "ctx"), None, "tp"),
        P(("fsdp", "ctx"), "tp"),
        P(None, "tp"),
        P(("fsdp", "ctx")),
        P(("fsdp", "ctx"), None),
        P(("fsdp", "ctx"), None, None, "tp"),
        P(("fsdp", "ctx"), None, "tp"),
        P("ctx", "fsdp", None, None),
        P("fsdp", "ctx", None),
    )
    return jax.shard_map(
        on_device,
        mesh=mesh,
        in_specs=placed,
        out_specs=(
            P("fsdp", "ctx", None),
            P("fsdp", "ctx", None),
            P(("fsdp", "ctx")),
            P(("fsdp", "ctx"), None, "tp"),
            P(("fsdp", "ctx"), "tp"),
            P(None, "tp"),
            P(("fsdp", "ctx")),
            P(("fsdp", "ctx"), None),
            P(("fsdp", "ctx"), None, None, "tp"),
            P(("fsdp", "ctx"), None, "tp"),
        ),
        check_vma=False,
    )
```

profile of v0, /device:TPU:0, one launch (start us, length us, event | category | flops | bytes accessed | tf_op | source)
XLA Modules:
  0.0 2206.6 jit_solution(5604651613465843333)
XLA Ops:
  8.6 22.6 %all-gather = bf16[8,1,256]{2,1,0:T(2,128)(2,1)S(1)} all-gather(bf16[1,1,256]{2,1,0:T(2,128)(2,1)S(1)} %reshape.832), channel_id=1, replica_groups=mesh['fsdp'=2,'ctx'=4,'tp'=4] {'fsdp','ctx'}, dimensions={0}, use_global_device_ids=true | all-gather | bytes 4608 | tf_op jit(solution)/shard_map/all_gather | solution.py:81
  33.5 78.4 %all-gather.9.cloned.1.call-done = bf16[2048,3,512]{2,0,1:T(8,128)(2,1)} async-done(((bf16[256,3,512]{2,0,1:T(8,128)(2,1)}), bf16[2048,3,512]{2,0,1:T(8,128)(2,1)}) %all-gather.9.cloned.1.call-update) | async-done | bytes 6291472 | tf_op jit(solution)/shard_map/all_gather | solution.py:82
  118.0 6.0 all-reduce.4
  131.8 21.5 all-gather.13.cloned.1.call-done
  158.5 26.7 %all-gather.11.cloned.1.call-done = bf16[1,1024,4,128]{1,3,2,0:T(8,128)(2,1)} async-done(((bf16[1,256,4,128]{1,3,2,0:T(8,128)(2,1)}), bf16[1,1024,4,128]{1,3,2,0:T(8,128)(2,1)}) %all-gather.11.cloned.1.call-update) | async-done | bytes 1048592 | tf_op jit(solution)/shard_map/all_gather | solution.py:113
  188.7 46.1 %all-gather.15.cloned.1.call-done = bf16[2048,512]{1,0:T(8,128)(2,1)} async-done(((bf16[256,512]{1,0:T(8,128)(2,1)}), bf16[2048,512]{1,0:T(8,128)(2,1)}) %all-gather.15.cloned.1.call-update) | async-done | bytes 2097168 | tf_op jit(solution)/shard_map/all_gather | solution.py:83
  252.7 18.0 all-gather.1
  277.3 7.2 gather_fusion.2
  284.5 30.8 %all_gather.37 = bf16[2048,8]{0,1:T(8,128)(2,1)S(1)} all-gather(bf16[256,8]{0,1:T(8,128)(2,1)S(1)} %copy-done.73), channel_id=1, replica_groups=mesh['fsdp'=2,'ctx'=4,'tp'=4] {'fsdp','ctx'}, dimensions={0}, use_global_device_ids=true | all-gather | bytes 36864 | tf_op jit(solution)/shard_map/all_gather | solution.py:85
  319.5 6.1 gather_fusion.1
  326.1 6.5 gather_fusion.4
  337.1 182.0 %all-gather.17.cloned.1.call-done = bf16[2048,2,8,256]{3,0,1,2:T(8,128)(2,1)} async-done(((bf16[256,2,8,256]{3,0,1,2:T(8,128)(2,1)}), bf16[2048,2,8,256]{3,0,1,2:T(8,128)(2,1)}) %all-gather.17.cloned.1.call-update) | async-done | bytes 16777232 | tf_op jit(solution)/shard_map/all_gather | solution.py:150
  519.1 11.7 fusion.16
  530.8 114.3 %all-gather.19.cloned.1.call-done = bf16[2048,8,256]{2,0,1:T(8,128)(2,1)} async-done(((bf16[256,8,256]{2,0,1:T(8,128)(2,1)}), bf16[2048,8,256]{2,0,1:T(8,128)(2,1)}) %all-gather.19.cloned.1.call-update) | async-done | bytes 8388624 | tf_op jit(solution)/shard_map/all_gather | solution.py:151
  645.2 10.0 fusion.51
  658.3 63.9 %while.29 = (s32[]{:T(128)}, f32[256,2048]{1,0:T(8,128)}, s32[8,160]{1,0:T(8,128)S(1)}, bf16[8,160,2,256]{3,1,2,0:T(8,128)(2,1)}, bf16[2048,2,8,256]{3,0,1,2:T(8,128)(2,1)}, /*index=5*/f32[8,160]{1,0:T(8,128)S(1)}, s32[]{:T(128)}) while((s32[]{:T(128)}, f32[256,2048]{1,0:T(8,128)}, s32[8,160]{1,0:T(8,128)S(1)}, ...), condition=%wide.region_24.25_spmd, body=%wide.region_22.24_spmd.sunk | while | flops 336200160 | bytes 7508829 | solution.py:219
  660.8 5.4 scatter_fusion
  668.8 5.4 scatter_fusion
  676.8 5.4 scatter_fusion
  684.8 5.4 scatter_fusion
  692.8 5.4 scatter_fusion
  708.7 5.4 scatter_fusion
  723.8 80.3 %while.28 = (s32[]{:T(128)}, f32[256,2048]{1,0:T(8,128)}, f32[8,160]{1,0:T(8,128)S(1)}, s32[8,160]{1,0:T(8,128)S(1)}, bf16[8,160,256]{2,1,0:T(8,128)(2,1)}, /*in...) while((s32[]{:T(128)}, f32[256,2048]{1,0:T(8,128)}, ...), condition=%wide.region_20.21_spmd, body=%wide.region_17.20_spmd.sunk | while | flops 169084224 | bytes 9793273 | solution.py:183
  728.3 5.5 scatter_custom_fusion.13
  738.3 5.6 scatter_custom_fusion.13
  748.4 5.5 scatter_custom_fusion.13
  758.4 5.6 scatter_custom_fusion.13
  768.5 5.5 scatter_custom_fusion.13
  778.5 5.5 scatter_custom_fusion.13
  788.5 5.5 scatter_custom_fusion.13
  798.5 5.5 scatter_custom_fusion.13
  804.2 6.2 gather_fusion.3
  810.5 25.5 %psum.75 = f32[256,4]{1,0:T(8,128)S(1)} all-reduce(f32[256,4]{1,0:T(8,128)S(1)} %reshape.775), channel_id=1, replica_groups=mesh['fsdp'=2,'ctx'=4,'tp'=4] {'tp'}, use_global_device_ids=true, to_apply=%region_26.27 | all-reduce | flops 1024 | bytes 8192 | tf_op jit(solution)/shard_map/psum | solution.py:236
  856.5 18.8 convolution_bitcast_fusion.1
  878.6 9.9 reduce-scatter.9.cloned.1.call-done
  890.5 43.5 %reduce-scatter.7.cloned.1.call-done = f32[1,256,4,128]{3,1,2,0:T(8,128)} async-done(((f32[1,1024,4,128]{3,1,2,0:T(8,128)}), f32[1,256,4,128]{3,1,2,0:T(8,128)}) %reduce-scatter.7.cloned.1.call-update) | async-done | bytes 524304 | tf_op jit(solution)/shard_map/reduce_scatter | solution.py:286
  938.5 6.5 all-reduce.3
  946.9 6.0 convolution_bitcast_fusion.3
  954.0 12.9 convolution_bitcast_fusion.2
  966.9 33.6 %pad_maximum_fusion = f32[2048,3,8,256]{0,3,1,2:T(8,128)} fusion(f32[2048,1,8,256]{0,3,1,2:T(8,128)} %convolution_bitcast_fusion.2, f32[2048,2,8,256]{0,3,1,2:T(8,128)} %convolution_bitcast_fusion.1), kind=kLoop, calls=%fused_computation.32 | loop fusion | flops 12582912 | bytes 100663296 | tf_op jit(solution)/shard_map/concatenate | solution.py:229
  1008.9 7.4 fusion.64
  1018.2 19.5 all-reduce.14.cloned.1.call-done
  1039.8 38.9 %all-reduce.2 = (f32[2048]{0:T(1024)S(1)}, f32[2,512]{1,0:T(2,128)}, f32[2048]{0:T(1024)S(1)}) all-reduce(f32[2048]{0:T(1024)S(1)} %get-tuple-element.336, f32[2,512]{1,0:T(2,128)S(1)} %pad_maximum_fusion.6, f32[2048]{0:T(1024)S(1)} %get-tuple-element.334), channel_id=4, replica_groups=mesh['fsdp'=2,'ctx'=4,'tp'=4] {'fsdp','ctx'}, use_global_device_ids=true, to_apply=%region_40.41.clone | all-reduce | flops 5120 | bytes 40960
  1085.0 747.3 %reduce-scatter.17.cloned.1.call-done = f32[256,3,8,256]{0,3,1,2:T(8,128)} async-done(((f32[2048,3,8,256]{0,3,1,2:T(8,128)}), f32[256,3,8,256]{0,3,1,2:T(8,128)}) %reduce-scatter.17.cloned.1.call-update) | async-done | bytes 6291472 | tf_op jit(solution)/shard_map/reduce_scatter | solution.py:228
  1836.8 5.5 copy.156
  1846.1 50.5 %reduce-scatter.15.cloned.1.call-done = f32[256,8]{0,1:T(8,128)} async-done(((f32[2048,8]{0,1:T(8,128)}), f32[256,8]{0,1:T(8,128)}) %reduce-scatter.15.cloned.1.call-update) | async-done | bytes 8208 | tf_op jit(solution)/shard_map/reduce_scatter | solution.py:324
  1896.6 91.0 %reduce-scatter.13.cloned.1.call-done = f32[256,512]{1,0:T(8,128)} async-done(((f32[2048,512]{1,0:T(8,128)}), f32[256,512]{1,0:T(8,128)}) %reduce-scatter.13.cloned.1.call-update) | async-done | bytes 524304 | tf_op jit(solution)/shard_map/reduce_scatter | solution.py:322
  1987.7 212.1 %reduce-scatter.11.cloned.1.call-done = f32[256,3,512]{2,0,1:T(8,128)} async-done(((f32[2048,3,512]{2,0,1:T(8,128)}), f32[256,3,512]{2,0,1:T(8,128)}) %reduce-scatter.11.cloned.1.call-update) | async-done | bytes 1572880 | tf_op jit(solution)/shard_map/reduce_scatter | solution.py:321
  (381 shorter events, 190.1 us)
Async XLA Ops:
  7.2 25.5 %copy-start.8 = (bf16[1,256,2048]{2,1,0:T(8,128)(2,1)S(1)}, bf16[1,256,2048]{2,1,0:T(8,128)(2,1)}, u32[]{:S(2)}) copy-start(bf16[1,256,2048]{2,1,0:T(8,128)(2,1)} %param.15) | copy-start | bytes 3145732
  7.2 26.3 %copy-start.68 = (bf16[2,512]{1,0:T(2,128)(2,1)S(1)}, bf16[2,512]{1,0:T(2,128)(2,1)}, u32[]{:S(2)}) copy-start(bf16[2,512]{1,0:T(2,128)(2,1)} %param.19) | copy-start | bytes 6148
  7.2 104.8 %all-gather.9.cloned.1.call-start = ((), (), s32[]{:S(2)}) async-start(), calls=%async_computation.6 | async-start | bytes 7077888 | tf_op jit(solution)/shard_map/all_gather | solution.py:82
  7.9 145.3 %all-gather.13.cloned.1.call-start = ((), (), s32[]{:S(2)}) async-start(), calls=%async_computation.8 | async-start | bytes 1310720 | tf_op jit(solution)/shard_map/all_gather | solution.py:112
  31.2 85.3 %copy-start.43 = (f32[8,1,256]{2,1,0:T(1,128)}, f32[8,1,256]{2,1,0:T(1,128)S(1)}, u32[]{:S(2)}) copy-start(f32[8,1,256]{2,1,0:T(1,128)S(1)} %convert_element_type.162) | copy-start | bytes 24580
  32.7 97.7 %copy-start.28 = (f32[256,128]{1,0:T(8,128)}, f32[256,128]{1,0:T(8,128)S(1)}, u32[]{:S(2)}) copy-start(f32[256,128]{1,0:T(8,128)S(1)} %get-tuple-element.404) | copy-start | bytes 393220
  32.7 97.8 %copy-start.26 = (f32[256,128]{1,0:T(8,128)}, f32[256,128]{1,0:T(8,128)S(1)}, u32[]{:S(2)}) copy-start(f32[256,128]{1,0:T(8,128)S(1)} %get-tuple-element.405) | copy-start | bytes 393220
  33.5 83.1 %copy-start.60 = (f32[256]{0:T(256)}, f32[256]{0:T(256)S(1)}, u32[]{:S(2)}) copy-start(f32[256]{0:T(256)S(1)} %get-tuple-element.411) | copy-start | bytes 3076
  33.5 92.6 %copy-start.50 = (f32[1,512]{1,0:T(1,128)}, f32[1,512]{1,0:T(1,128)S(1)}, u32[]{:S(2)}) copy-start(f32[1,512]{1,0:T(1,128)S(1)} %get-tuple-element.408) | copy-start | bytes 6148
  33.5 98.1 %copy-start.52 = (f32[1,512]{1,0:T(1,128)}, f32[1,512]{1,0:T(1,128)S(1)}, u32[]{:S(2)}) copy-start(f32[1,512]{1,0:T(1,128)S(1)} %get-tuple-element.409) | copy-start | bytes 6148
  116.6 10.6 copy-start.12
  127.1 58.0 %all-gather.11.cloned.1.call-start = ((), (), s32[]{:S(2)}) async-start(), calls=%async_computation.7 | async-start | bytes 1310720 | tf_op jit(solution)/shard_map/all_gather | solution.py:113
  129.7 105.0 %all-gather.15.cloned.1.call-start = ((), (), s32[]{:S(2)}) async-start(), calls=%async_computation.9 | async-start | bytes 2359296 | tf_op jit(solution)/shard_map/all_gather | solution.py:83
  130.3 185.7 %all-reduce.10.cloned.1.call-start = ((), (), s32[]{:S(2)}) async-start(), calls=%async_computation.10 | async-start | bytes 4194304 | tf_op jit(solution)/shard_map/psum | solution.py:135
  130.8 24.6 %copy-start.14 = (f32[256,1,512]{0,2,1:T(8,128)}, f32[256,1,512]{0,2,1:T(8,128)S(1)}, u32[]{:S(2)}) copy-start(f32[256,1,512]{0,2,1:T(8,128)S(1)} %copy.166) | copy-start | bytes 1572868
  131.4 24.0 %copy-start.58 = (f32[256]{0:T(256)}, f32[256]{0:T(256)S(1)}, u32[]{:S(2)}) copy-start(f32[256]{0:T(256)S(1)} %get-tuple-element.413) | copy-start | bytes 3076
  131.8 23.6 %copy-start.24 = (bf16[256,4,128]{0,2,1:T(8,128)(2,1)}, bf16[256,4,128]{0,2,1:T(8,128)(2,1)S(1)}, u32[]{:S(2)}) copy-start(bf16[256,4,128]{0,2,1:T(8,128)(2,1)S(1)} %fusion.55) | copy-start | bytes 786436
  188.7 46.1 %copy-start.37 = (bf16[4,128,256]{2,1,0:T(8,128)(2,1)}, bf16[4,128,256]{2,1,0:T(8,128)(2,1)S(1)}, u32[]{:S(2)}) copy-start(bf16[4,128,256]{2,1,0:T(8,128)(2,1)S(1)} %fusion.42) | copy-start | bytes 786436
  238.5 280.7 %all-gather.17.cloned.1.call-start = ((), (), s32[]{:S(2)}) async-start(), calls=%async_computation.11 | async-start | bytes 18874368 | tf_op jit(solution)/shard_map/all_gather | solution.py:150
  242.1 10.6 copy-start.74
  242.1 403.1 %all-gather.19.cloned.1.call-start = ((), (), s32[]{:S(2)}) async-start(), calls=%async_computation.12 | async-start | bytes 9437184 | tf_op jit(solution)/shard_map/all_gather | solution.py:151
  244.6 591.7 %all-reduce.12.cloned.1.call-start = ((), (), s32[]{:S(2)}) async-start(), calls=%async_computation.13 | async-start | bytes 4194304 | tf_op jit(solution)/shard_map/psum | solution.py:236
  270.7 47.9 %copy-start.45 = (f32[8,1,256]{2,1,0:T(1,128)}, f32[8,1,256]{2,1,0:T(1,128)S(1)}, u32[]{:S(2)}) copy-start(f32[8,1,256]{2,1,0:T(1,128)S(1)} %convert_element_type.163) | copy-start | bytes 24580
  315.4 10.3 copy-start.41
  722.2 166.4 %reduce-scatter.9.cloned.1.call-start = ((), (), s32[]{:S(2)}) async-start(), calls=%async_computation.15 | async-start | bytes 2621440 | tf_op jit(solution)/shard_map/reduce_scatter | solution.py:287
  804.2 32.0 %copy-start.55 = (s32[1,1,256,4]{2,3,1,0:T(4,128)S(1)}, s32[1,1,256,4]{2,3,1,0:T(4,128)}, u32[]{:S(2)}) copy-start(s32[1,1,256,4]{2,3,1,0:T(4,128)} %param.24) | copy-start | bytes 12292
  804.2 32.0 %copy-start.48 = (f32[256,8]{0,1:T(8,128)S(1)}, f32[256,8]{0,1:T(8,128)}, u32[]{:S(2)}) copy-start(f32[256,8]{0,1:T(8,128)} %copy-done.47) | copy-start | bytes 24580
  804.2 32.0 %copy-start.65 = (f32[256]{0:T(256)S(1)}, f32[256]{0:T(256)}, u32[]{:S(2)}) copy-start(f32[256]{0:T(256)} %copy-done.64) | copy-start | bytes 3076
  804.2 32.0 %copy-start.67 = (f32[256]{0:T(256)S(1)}, f32[256]{0:T(256)}, u32[]{:S(2)}) copy-start(f32[256]{0:T(256)} %copy-done.66) | copy-start | bytes 3076
  804.2 32.1 %copy-start.5 = (f32[256,2048]{1,0:T(8,128)S(1)}, f32[256,2048]{1,0:T(8,128)}, u32[]{:S(2)}) copy-start(f32[256,2048]{1,0:T(8,128)} %copy-done.4) | copy-start | bytes 6291460
  804.2 32.1 %copy-start.42 = (bf16[2048,8]{0,1:T(8,128)(2,1)S(1)}, bf16[2048,8]{0,1:T(8,128)(2,1)}, u32[]{:S(2)}) copy-start(bf16[2048,8]{0,1:T(8,128)(2,1)} %copy-done.41) | copy-start | bytes 98308
  804.2 32.1 %copy-start.46 = (f32[8,1,256]{2,1,0:T(1,128)S(1)}, f32[8,1,256]{2,1,0:T(1,128)}, u32[]{:S(2)}) copy-start(f32[8,1,256]{2,1,0:T(1,128)} %copy-done.45) | copy-start | bytes 24580
  804.2 32.1 %copy-start.63 = (f32[256]{0:T(256)S(1)}, f32[256]{0:T(256)}, u32[]{:S(2)}) copy-start(f32[256]{0:T(256)} %copy-done.62) | copy-start | bytes 3076
  846.9 87.2 %reduce-scatter.7.cloned.1.call-start = ((), (), s32[]{:S(2)}) async-start(), calls=%async_computation.14 | async-start | bytes 2621440 | tf_op jit(solution)/shard_map/reduce_scatter | solution.py:286
  855.3 182.4 %all-reduce.14.cloned.1.call-start = ((), (), s32[]{:S(2)}) async-start(), calls=%async_computation.20 | async-start | bytes 8388608 | tf_op jit(solution)/shard_map/psum | solution.py:190
  856.5 18.8 copy-start.11
  856.5 18.9 copy-start.20
  876.6 57.4 %copy-start.29 = (f32[256,128]{1,0:T(8,128)S(1)}, f32[256,128]{1,0:T(8,128)}, u32[]{:S(2)}) copy-start(f32[256,128]{1,0:T(8,128)} %copy-done.28) | copy-start | bytes 393220
  889.6 45.8 %copy-start.18 = (f32[1,256,4,128]{3,2,1,0:T(4,128)S(1)}, f32[1,256,4,128]{3,2,1,0:T(4,128)}, u32[]{:S(2)}) copy-start(f32[1,256,4,128]{3,2,1,0:T(4,128)} %copy-done.17) | copy-start | bytes 1572868
  889.6 45.8 %copy-start.27 = (f32[256,128]{1,0:T(8,128)S(1)}, f32[256,128]{1,0:T(8,128)}, u32[]{:S(2)}) copy-start(f32[256,128]{1,0:T(8,128)} %copy-done.26) | copy-start | bytes 393220
  889.6 45.8 %copy-start.57 = (f32[256]{0:T(256)S(1)}, f32[256]{0:T(256)}, u32[]{:S(2)}) copy-start(f32[256]{0:T(256)} %copy-done.56) | copy-start | bytes 3076
  935.7 9.4 copy-start.70
  935.7 9.4 copy-start.71
  938.5 8.4 copy-start.36
  953.0 879.3 %reduce-scatter.17.cloned.1.call-start = ((), (), s32[]{:S(2)}) async-start(), calls=%async_computation.19 | async-start | bytes 56623104 | tf_op jit(solution)/shard_map/reduce_scatter | solution.py:228
  1000.6 896.1 %reduce-scatter.15.cloned.1.call-start = ((), (), s32[]{:S(2)}) async-start(), calls=%async_computation.18 | async-start | bytes 73728 | tf_op jit(solution)/shard_map/reduce_scatter | solution.py:324
  1003.1 984.6 %reduce-scatter.13.cloned.1.call-start = ((), (), s32[]{:S(2)}) async-start(), calls=%async_computation.17 | async-start | bytes 4718592 | tf_op jit(solution)/shard_map/reduce_scatter | solution.py:322
  1007.7 1192.1 %reduce-scatter.11.cloned.1.call-start = ((), (), s32[]{:S(2)}) async-start(), calls=%async_computation.16 | async-start | bytes 14155776 | tf_op jit(solution)/shard_map/reduce_scatter | solution.py:321
  (43 other events, 110.3 us)
Sparse Core Ops, SparseCore 0:
  10.2 101.7 all-gather.8
  127.2 25.9 all-gather.12
  155.4 29.6 all-gather.10
  187.1 47.5 all-gather.14
  238.6 49.8 all-reduce.9
  291.3 227.7 all-gather.16
  522.0 123.1 all-gather.18
  722.3 49.5 all-reduce.11
  847.0 41.5 reduce-scatter.8
  890.8 43.1 reduce-scatter.6
  953.1 84.5 all-reduce.13
  1041.9 790.2 reduce-scatter.16
  1836.2 60.3 reduce-scatter.14
  1900.7 86.9 reduce-scatter.12
  1992.1 207.5 reduce-scatter.10
where the time goes:
time: 2220 us; the launch traced here: 2210 us
  waiting for transfers between devices  1640 us (74%)
  other arithmetic  150 us (7%)
  blocking collectives  148 us (7%)
  matrix products  141 us (6%)
  local copies, waits for them, and re-layouts  106 us (5%)
    reduce_scatter x1, waiting for transfers between devices, on_device(): lax.psum_scatter(jnp.concatenate([gate_up_term, down_term[:, None]], axis...  747 us
    reduce_scatter x1, waiting for transfers between devices, on_device(): lax.psum_scatter(grad_qkv, ('fsdp', 'ctx'), scatter_dimension=0, tiled=True)  212 us
    all_gather x1, waiting for transfers between devices, on_device(): lax.all_gather(gate_up_weight, ('fsdp', 'ctx'), axis=0, tiled=True)  182 us
    all_gather x1, waiting for transfers between devices, on_device(): lax.all_gather(down_weight, ('fsdp', 'ctx'), axis=0, tiled=True)  114 us
    reduce_scatter x1, waiting for transfers between devices, on_device(): lax.psum_scatter(grad_out, ('fsdp', 'ctx'), scatter_dimension=0, tiled=True)  91 us
    all_gather x1, waiting for transfers between devices, on_device(): lax.all_gather(qkv_weight, ('fsdp', 'ctx'), axis=0, tiled=True)  78.4 us
    reduce_scatter x1, waiting for transfers between devices, on_device(): lax.psum_scatter(grad_router, ('fsdp', 'ctx'), scatter_dimension=0, tiled...  50.5 us
    all_gather x1, waiting for transfers between devices, on_device(): lax.all_gather(out_weight, ('fsdp', 'ctx'), axis=0, tiled=True)  46.1 us
  transfers between devices with their start and end apart: 15, of which 13 were waited for; matrix products, arithmetic and copies ran while one was open for 12% of the time, Pallas kernels for 0%

commit v1 on v0

--- a/solution.py
+++ b/solution.py
@@ -337,7 +337,276 @@
     )
 
 
+def attend_scores(query_rot, key_rot, scale, block):
+    scores = jnp.einsum("qd,kd->qk", query_rot, key_rot, preferred_element_type=jnp.float32) * scale
+    length = scores.shape[0]
+    place = jnp.arange(length, dtype=jnp.int32) // block
+    return jnp.where(place[None, :] <= place[:, None], scores, -1e30)
+
+
+def by_head(
+    sizes,
+    inputs,
+    attn_gain,
+    qkv_weight,
+    out_weight,
+    qk_gains,
+    mlp_gain,
+    router_weight,
+    gate_up_weight,
+    down_weight,
+    routes,
+    cotangent,
+):
+    n_fsdp, n_ctx, n_tp = sizes
+    places = n_fsdp * n_ctx
+    both = ("fsdp", "ctx")
+    f32, bf16 = jnp.float32, jnp.bfloat16
+    _, block, width = inputs.shape
+    depth = width // places
+    quarter = width // n_tp
+    length = n_ctx * block
+    hidden = gate_up_weight.shape[3]
+    scale = 1.0 / math.sqrt(HEAD_DIM)
+    ctx, tp = lax.axis_index("ctx"), lax.axis_index("tp")
+
+    def own_quarter(values):
+        return lax.dynamic_slice_in_dim(values, tp * quarter, quarter, axis=1)
+
+    attn_scale = attn_gain.astype(f32)
+    mlp_scale = mlp_gain.astype(f32)
+    qkv_raw = qkv_weight.reshape(depth, 3, n_ctx, HEAD_DIM).transpose(2, 0, 1, 3)
+    qkv_raw = qkv_raw.reshape(n_ctx, depth, 3 * HEAD_DIM).astype(f32)
+    qkv_scaled = (qkv_raw * attn_scale[None, :, None]).astype(bf16)
+    head_weight = lax.all_to_all(qkv_scaled, "ctx", 0, 0, tiled=True)
+    head_weight = lax.all_gather(head_weight, "fsdp", axis=0, tiled=True)
+    head_weight = head_weight.reshape(width, 3 * HEAD_DIM)
+    gate_up_raw = gate_up_weight.transpose(2, 0, 1, 3).reshape(EXPERTS, depth, 2 * hidden)
+    down_raw = down_weight.transpose(1, 0, 2)
+    expert_send = jnp.concatenate(
+        [(gate_up_raw.astype(f32) * mlp_scale[None, :, None]).astype(bf16), down_raw], axis=2
+    )
+    expert_weight = lax.all_to_all(expert_send, both, 0, 0, tiled=True)
+    expert_weight = expert_weight.reshape(width, 3 * hidden)
+    gate_up_full = expert_weight[:, : 2 * hidden]
+    down_full = expert_weight[:, 2 * hidden :]
+    out_all = lax.all_gather(out_weight, both, axis=0, tiled=True)
+    router_f32 = router_weight.astype(f32)
+    router_all = lax.all_gather(router_f32 * mlp_scale[:, None], both, axis=0, tiled=True)
+    router_part = lax.dynamic_slice_in_dim(router_all, tp * quarter, quarter, axis=0)
+
+    routed = routes.reshape(block, TOPK)
+    named = (routed[:, :, None] == jnp.arange(EXPERTS, dtype=jnp.int32)).astype(f32).sum(axis=1)
+    order = jnp.arange(block, dtype=jnp.int32)
+    before = (order[None, :] < order[:, None]).astype(bf16)
+    earlier = jnp.dot(before, named.astype(bf16), preferred_element_type=f32).astype(jnp.int32)
+    slot_of = jnp.where(named > 0, earlier, -1)
+    picks = slot_of.T[:, None, :] == jnp.arange(CAP, dtype=jnp.int32)[None, :, None]
+    pick_f32 = picks.astype(f32)
+    pick = picks.astype(bf16).reshape(EXPERTS * CAP, block)
+
+    def dispatch(part):
+        rows = jnp.dot(pick, part, preferred_element_type=f32).astype(bf16)
+        rows = lax.all_to_all(rows.reshape(EXPERTS, CAP, quarter), both, 0, 0, tiled=True)
+        rows = lax.all_gather(rows, "tp", axis=2, tiled=True)
+        return rows.reshape(EXPERTS * CAP, width)
+
+    def bring_back(rows):
+        rows = lax.psum_scatter(
+            rows.reshape(EXPERTS, CAP, width), "tp", scatter_dimension=2, tiled=True
+        )
+        rows = lax.all_to_all(rows, both, 0, 0, tiled=True).reshape(EXPERTS * CAP, quarter)
+        return lax.dot_general(pick, rows, (((0,), (0,)), ((), ())), preferred_element_type=f32)
+
+    upstream_part = own_quarter(cotangent.reshape(block, width))
+    up_rows = dispatch(upstream_part)
+    upstream_part = upstream_part.astype(f32)
+
+    flat_in = inputs.reshape(block, width).astype(f32)
+    first_rms = inv_rms(flat_in)
+    in_part = own_quarter(flat_in)
+    normed_own = (flat_in * first_rms).astype(bf16)
+    share = block // n_tp
+    normed_share = lax.dynamic_slice_in_dim(normed_own, tp * share, share, axis=0)
+    normed = lax.all_gather(normed_share, ("ctx", "tp"), axis=0, tiled=True)
+    projected = jnp.dot(normed, head_weight, preferred_element_type=f32)
+    query_proj = projected[:, :HEAD_DIM]
+    key_proj = projected[:, HEAD_DIM : 2 * HEAD_DIM]
+    value_heads = projected[:, 2 * HEAD_DIM :].astype(bf16)
+    sums = lax.psum(
+        jnp.stack([jnp.sum(query_proj * query_proj, axis=-1), jnp.sum(key_proj * key_proj, axis=-1)]),
+        ("ctx", "tp"),
+    )
+    query_rms = lax.rsqrt(sums[0] / HQ + epsilon)[:, None]
+    key_rms = lax.rsqrt(sums[1] / HQ + epsilon)[:, None]
+    own_gains = lax.dynamic_slice_in_dim(qk_gains, ctx * HEAD_DIM, HEAD_DIM, axis=1).astype(f32)
+    query_gain, key_gain = own_gains[0], own_gains[1]
+    cosine, sine_table = rotary_tables(0, length)
+    query_rot = rotate(query_proj * query_rms * query_gain, cosine, sine_table).astype(bf16)
+    key_rot = rotate(key_proj * key_rms * key_gain, cosine, sine_table).astype(bf16)
+    scores = attend_scores(query_rot, key_rot, scale, block)
+    exponent = jnp.exp(scores - jnp.max(scores, axis=-1, keepdims=True))
+    probs = exponent / jnp.sum(exponent, axis=-1, keepdims=True)
+    probs_low = probs.astype(bf16)
+    attended = jnp.dot(probs_low, value_heads, preferred_element_type=f32).astype(bf16)
+    attended = lax.all_to_all(attended.reshape(n_ctx, block, HEAD_DIM), "ctx", 0, 0, tiled=True)
+    attended = attended.transpose(1, 0, 2).reshape(block, n_ctx * HEAD_DIM)
+    branch = jnp.einsum("th,dh->td", attended, out_all, preferred_element_type=f32)
+    branch = lax.psum_scatter(branch.astype(bf16), "tp", scatter_dimension=1, tiled=True)
+    middle = in_part + branch.astype(f32)
+
+    small = jnp.concatenate(
+        [
+            jnp.dot(middle, router_part, precision=highest),
+            jnp.sum(middle * middle, axis=-1, keepdims=True),
+        ],
+        axis=1,
+    )
+    small = lax.psum(small, "tp")
+    raw_logits = small[:, :EXPERTS]
+    second_rms = lax.rsqrt(small[:, EXPERTS:] / width + epsilon)
+    chances = jax.nn.softmax(raw_logits * second_rms, axis=-1)
+    normed_mlp = (middle * second_rms).astype(bf16)
+    rows = dispatch(normed_mlp)
+    slot_gates = jnp.sum(pick_f32 * chances.T[:, None, :], axis=-1)
+    slot_gates = lax.all_to_all(slot_gates, both, 0, 0, tiled=True).reshape(EXPERTS * CAP, 1)
+
+    gate_up = jnp.dot(rows, gate_up_full, preferred_element_type=f32)
+    gate_part, up_part = gate_up[:, :hidden], gate_up[:, hidden:]
+    sigmoid = jax.nn.sigmoid(gate_part)
+    silu = gate_part * sigmoid
+    activated = silu * up_part
+    act_low = (activated * slot_gates).astype(bf16)
+    act_grads = jnp.dot(up_rows, down_full, preferred_element_type=f32)
+    slot_products = jnp.sum(activated * act_grads, axis=-1)
+    gated = act_grads * slot_gates
+    pre_grads = jnp.concatenate(
+        [gated * up_part * sigmoid * (1.0 + gate_part * (1.0 - sigmoid)), gated * silu], axis=1
+    ).astype(bf16)
+    back_rows = lax.dot_general(
+        pre_grads, gate_up_full, (((1,), (1,)), ((), ())), preferred_element_type=f32
+    )
+    back_part = bring_back(back_rows.astype(bf16))
+    returned = lax.dot_general(
+        act_low, down_full, (((1,), (1,)), ((), ())), preferred_element_type=f32
+    )
+    output_part = (middle + bring_back(returned.astype(bf16))).astype(bf16)
+    rows_in = (((0,), (0,)), ((), ()))
+    expert_grads = jnp.concatenate(
+        [
+            lax.dot_general(rows, pre_grads, rows_in, preferred_element_type=f32),
+            lax.dot_general(up_rows, act_low, rows_in, preferred_element_type=f32),
+        ],
+        axis=1,
+    ).astype(bf16)
+    expert_grads = lax.all_to_all(
+        expert_grads.reshape(EXPERTS, depth, 3 * hidden), both, 0, 0, tiled=True
+    ).astype(f32)
+    slot_products = lax.psum(slot_products, "tp").reshape(EXPERTS, CAP)
+    slot_products = lax.all_to_all(slot_products, both, 0, 0, tiled=True)
+
+    chance_grads = jnp.sum(pick_f32 * slot_products[:, :, None], axis=1).T
+    logit_grads = chances * (chance_grads - jnp.sum(chances * chance_grads, axis=-1, keepdims=True))
+    scaled_mlp = back_part + jnp.dot(logit_grads, router_part.T, precision=highest)
+    inner = lax.psum(jnp.sum(scaled_mlp * middle, axis=-1, keepdims=True), "tp")
+    middle_grad = upstream_part + second_rms * scaled_mlp - middle * second_rms**3 / width * inner
+    router_term = lax.dot_general(
+        normed_mlp.astype(f32), logit_grads, rows_in, precision=highest
+    )
+    router_term = lax.all_gather(router_term, "tp", axis=0, tiled=True)
+    router_term = lax.psum_scatter(router_term, both, scatter_dimension=0, tiled=True)
+    grad_router = router_term * mlp_scale[:, None]
+
+    branch_grad = lax.all_gather(middle_grad.astype(bf16), "tp", axis=1, tiled=True)
+    grad_out = lax.dot_general(branch_grad, attended, rows_in, preferred_element_type=f32)
+    grad_out = lax.psum_scatter(grad_out.astype(bf16), both, scatter_dimension=0, tiled=True)
+    attended_grad = jnp.dot(branch_grad, out_all, preferred_element_type=f32).astype(bf16)
+    attended_grad = attended_grad.reshape(block, n_ctx, HEAD_DIM).transpose(1, 0, 2)
+    attended_grad = lax.all_to_all(attended_grad, "ctx", 0, 0, tiled=True)
+    attended_grad = attended_grad.reshape(length, HEAD_DIM)
+    prob_grads = jnp.einsum(
+        "qd,kd->qk", attended_grad, value_heads, preferred_element_type=f32
+    )
+    score_grads = (
+        probs * (prob_grads - jnp.sum(probs * prob_grads, axis=-1, keepdims=True))
+    ).astype(bf16)
+    query_grads = jnp.dot(score_grads, key_rot, preferred_element_type=f32) * scale
+    key_grads = lax.dot_general(score_grads, query_rot, rows_in, preferred_element_type=f32) * scale
+    value_grads = lax.dot_general(probs_low, attended_grad, rows_in, preferred_element_type=f32)
+    query_norm_grad = rotate_back(query_grads, cosine, sine_table)
+    key_norm_grad = rotate_back(key_grads, cosine, sine_table)
+    query_scaled = query_norm_grad * query_gain
+    key_scaled = key_norm_grad * key_gain
+    inners = lax.psum(
+        jnp.stack([jnp.sum(query_scaled * query_proj, axis=-1), jnp.sum(key_scaled * key_proj, axis=-1)]),
+        ("ctx", "tp"),
+    )
+    query_pre = query_rms * query_scaled - query_proj * query_rms**3 / HQ * inners[0][:, None]
+    key_pre = key_rms * key_scaled - key_proj * key_rms**3 / HQ * inners[1][:, None]
+    gain_terms = jnp.stack(
+        [
+            jnp.sum(query_norm_grad * query_proj * query_rms, axis=0),
+            jnp.sum(key_norm_grad * key_proj * key_rms, axis=0),
+        ]
+    )
+    gain_terms = lax.all_gather(lax.psum(gain_terms, "fsdp"), "ctx", axis=1, tiled=True)
+    proj_grads = jnp.concatenate([query_pre, key_pre, value_grads], axis=1).astype(bf16)
+    qkv_grads = lax.dot_general(normed, proj_grads, rows_in, preferred_element_type=f32)
+    qkv_grads = lax.all_to_all(
+        qkv_grads.astype(bf16).reshape(places, depth, 3 * HEAD_DIM), both, 0, 0, tiled=True
+    )
+    qkv_grads = qkv_grads.astype(f32).reshape(n_fsdp, n_ctx, depth, 3 * HEAD_DIM).sum(axis=0)
+    grad_qkv = (qkv_grads * attn_scale[None, :, None]).reshape(n_ctx, depth, 3, HEAD_DIM)
+    grad_qkv = grad_qkv.transpose(1, 2, 0, 3).reshape(depth, 3, n_ctx * HEAD_DIM)
+    scaled_first = lax.dot_general(
+        proj_grads, head_weight, (((1,), (1,)), ((), ())), preferred_element_type=f32
+    ).astype(bf16)
+    scaled_first = lax.psum_scatter(scaled_first, "tp", scatter_dimension=1, tiled=True)
+    scaled_first = lax.psum_scatter(scaled_first, "ctx", scatter_dimension=0, tiled=True)
+    scaled_first = scaled_first.astype(f32)
+    gains = jnp.stack(
+        [
+            jnp.sum(qkv_grads * qkv_raw, axis=(0, 2)),
+            jnp.sum(expert_grads[:, :, : 2 * hidden] * gate_up_raw.astype(f32), axis=(0, 2)),
+        ]
+    )
+    last_inner = jnp.sum(scaled_first * in_part, axis=-1)
+    gains, last_inner = lax.psum((gains, last_inner), "tp")
+    grad_mlp_gain = gains[1] + jnp.sum(router_term * router_f32, axis=-1)
+    grad_inputs = (
+        middle_grad
+        + first_rms * scaled_first
+        - in_part * first_rms**3 / width * last_inner[:, None]
+    )
+    grad_inputs = lax.all_gather(grad_inputs.astype(bf16), "tp", axis=1, tiled=True).astype(f32)
+    output = lax.all_gather(output_part, "tp", axis=1, tiled=True)
+    grad_gate_up = (expert_grads[:, :, : 2 * hidden] * mlp_scale[None, :, None]).reshape(
+        EXPERTS, depth, 2, hidden
+    )
+    return (
+        output[None],
+        grad_inputs[None],
+        gains[0],
+        grad_qkv,
+        grad_out.astype(f32),
+        gain_terms,
+        grad_mlp_gain,
+        grad_router,
+        grad_gate_up.transpose(1, 2, 0, 3),
+        expert_grads[:, :, 2 * hidden :].transpose(1, 0, 2),
+    )
+
+
 def solution(mesh):
+    sizes = (mesh.shape["fsdp"], mesh.shape["ctx"], mesh.shape["tp"])
+    one_expert = sizes[0] * sizes[1] == EXPERTS
+    one_head = sizes[1] * sizes[2] * HEAD_DIM == HQ
+
+    def step(*arrays):
+        if one_expert and one_head and arrays[0].shape[0] == 1:
+            return by_head(sizes, *arrays)
+        return on_device(*arrays)
+
     placed = (
         P("fsdp", "ctx", None),
         P(("fsdp", "ctx")),
@@ -352,7 +621,7 @@
         P("fsdp", "ctx", None),
     )
     return jax.shard_map(
-        on_device,
+        step,
         mesh=mesh,
         in_specs=placed,
         out_specs=(

time: 2220 us -> 952 us (0.43)
  waiting for transfers between devices: 1640 us -> 444 us
  blocking collectives: 148 us -> 249 us
  other arithmetic: 150 us -> 53.2 us
  matrix products: 141 us -> 77.7 us
  local copies, waits for them, and re-layouts: 106 us -> 66.8 us
  starting transfers between devices: 0.83 us -> 34.7 us
    reduce_scatter x6 -> x7, waiting for transfers between devices: 1150 us -> 119 us  [the longest x1 54.2 us: by_head(): lax.psum_scatter(grad_out.astype(bf16), both, scatter_dimension=0, tiled=...]
    all_gather x6 -> x8, waiting for transfers between devices: 469 us -> 98.1 us  [the longest x1 53.3 us: by_head(): normed = lax.all_gather(normed_share, ('ctx', 'tp'), axis=0, tiled=True)]
    all_to_all x0 -> x8, waiting for transfers between devices: none -> 226 us  [the longest x1 70.7 us: by_head(): expert_weight = lax.all_to_all(expert_send, both, 0, 0, tiled=True)]
    all_to_all x0 -> x4, blocking collectives: none -> 104 us  [the longest x2 68.4 us: dispatch(): lax.all_to_all(rows.reshape(EXPERTS, CAP, quarter), both, 0, 0, tiled=True)]
    scatter-add x16 -> x0, other arithmetic: 87.9 us -> none  [the longest x8 44.4 us: expert_forward(): combined.at[expert_tokens].add(returned_rows * expert_gates[:, None])]
    dot_general x35 -> x26, matrix products: 141 us -> 77.7 us  [the longest x1 7.58 us: by_head(): gate_up = jnp.dot(rows, gate_up_full, preferred_element_type=f32)]
    psum x3 -> x7, blocking collectives: 38.1 us -> 97.9 us  [the longest x1 32.4 us: by_head(): lax.psum(jnp.stack([jnp.sum(query_proj * query_proj, axis=-1), jnp.sum(ke...]
    gather x14 -> x0, local copies, waits for them, and re-layouts: 43.3 us -> none  [the longest x8 17.1 us: expert_forward(): products = jnp.sum(returned_rows * upstream[expert_tokens], axis=-1)]
  transfers between devices with their start and end apart: 15 -> 23, of which waited for: 13 -> 16; matrix products, arithmetic and copies ran while one was open for 12% -> 16% of each run, Pallas kernels for 0% -> 0%
where the time goes in v1:
time: 952 us; the launch traced here: 941 us
  waiting for transfers between devices  444 us (47%)
  blocking collectives  249 us (26%)
  matrix products  77.7 us (8%)
  local copies, waits for them, and re-layouts  66.8 us (7%)
  other arithmetic  53.2 us (6%)
  starting transfers between devices  34.7 us (4%)
  between operations  15.5 us (2%)
    all_to_all x1, waiting for transfers between devices, by_head(): expert_weight = lax.all_to_all(expert_send, both, 0, 0, tiled=True)  70.7 us
    all_to_all x1, waiting for transfers between devices, by_head(): lax.all_to_all(expert_grads.reshape(EXPERTS, depth, 3 * hidden), both, 0,...  69 us
    all_to_all x2, blocking collectives, dispatch(): lax.all_to_all(rows.reshape(EXPERTS, CAP, quarter), both, 0, 0, tiled=True)  68.4 us
    reduce_scatter x1, waiting for transfers between devices, by_head(): lax.psum_scatter(grad_out.astype(bf16), both, scatter_dimension=0, tiled=...  54.2 us
    all_gather x1, waiting for transfers between devices, by_head(): normed = lax.all_gather(normed_share, ('ctx', 'tp'), axis=0, tiled=True)  53.3 us
    reduce_scatter x2, waiting for transfers between devices, bring_back(): lax.psum_scatter(rows.reshape(EXPERTS, CAP, width), 'tp', scatter_dimensi...  49.1 us
    all_to_all x2, waiting for transfers between devices, bring_back(): lax.all_to_all(rows, both, 0, 0, tiled=True).reshape(EXPERTS * CAP, quarter)  36.9 us
    psum x1, blocking collectives, by_head(): lax.psum(jnp.stack([jnp.sum(query_proj * query_proj, axis=-1), jnp.sum(ke...  32.4 us
  transfers between devices with their start and end apart: 23, of which 16 were waited for; matrix products, arithmetic and copies ran while one was open for 16% of the time, Pallas kernels for 0%

profile of v1, /device:TPU:0, one launch (start us, length us, event | category | flops | bytes accessed | tf_op | source)
XLA Modules:
  0.0 940.9 jit_solution(4810003720874785450)
XLA Ops:
  10.0 26.5 %all_to_all.68 = bf16[4,256,384]{1,2,0:T(8,128)(2,1)} all-to-all(bf16[4,256,384]{1,2,0:T(8,128)(2,1)S(1)} %fusion.6), channel_id=1, replica_groups=mesh['fsdp'=2,'ctx'=4,'tp'=4] {'ctx'}, dimensions={0} | all-to-all | bytes 1572864 | tf_op jit(solution)/shard_map/all_to_all | solution.py:381
  43.8 21.5 %all-gather.11.cloned.1.call-done = bf16[8,256,384]{2,1,0:T(8,128)(2,1)} async-done(((bf16[4,256,384]{2,1,0:T(8,128)(2,1)}), bf16[8,256,384]{2,1,0:T(8,128)(2,1)}) %all-gather.11.cloned.1.call-update) | async-done | bytes 1572880 | tf_op jit(solution)/shard_map/all_gather | solution.py:382
  65.3 53.3 %all-gather.9.cloned.1.call-done = bf16[1024,2048]{1,0:T(8,128)(2,1)} async-done(((bf16[64,2048]{1,0:T(8,128)(2,1)}), bf16[1024,2048]{1,0:T(8,128)(2,1)}) %all-gather.9.cloned.1.call-update) | async-done | bytes 4194320 | tf_op jit(solution)/shard_map/all_gather | solution.py:431
  118.6 4.5 fusion.92
  123.2 32.4 %psum.56 = f32[2,1024]{1,0:T(2,128)S(1)} all-reduce(f32[2,1024]{1,0:T(2,128)S(1)} %pad_maximum_fusion.10), channel_id=1, replica_groups=mesh['fsdp'=2,'ctx'=4,'tp'=4] {'ctx','tp'}, use_global_device_ids=true, to_apply=%region_3.4 | all-reduce | flops 2048 | bytes 16384 | tf_op jit(solution)/shard_map/psum | solution.py:436
  168.9 6.7 all-to-all-done.1
  179.7 30.6 %all_gather.36 = f32[2048,8]{0,1:T(8,128)S(1)} all-gather(f32[256,8]{0,1:T(8,128)S(1)} %convert_multiply_fusion.3), channel_id=1, replica_groups=mesh['fsdp'=2,'ctx'=4,'tp'=4] {'fsdp','ctx'}, dimensions={0}, use_global_device_ids=true | all-gather | bytes 73728 | tf_op jit(solution)/shard_map/all_gather | solution.py:395
  212.1 10.1 %psum.57 = f32[256,9]{0,1:T(8,128)S(1)} all-reduce(f32[256,9]{0,1:T(8,128)S(1)} %pad_maximum_fusion.9), channel_id=1, replica_groups=mesh['fsdp'=2,'ctx'=4,'tp'=4] {'tp'}, use_global_device_ids=true, to_apply=%region_9.10 | all-reduce | flops 2304 | bytes 18432 | tf_op jit(solution)/shard_map/psum | solution.py:465
  223.4 34.6 %all_to_all.69 = bf16[8,160,512]{2,1,0:T(8,128)(2,1)} all-to-all(bf16[8,160,512]{2,1,0:T(8,128)(2,1)S(1)} %bitcast.177), channel_id=1, replica_groups=mesh['fsdp'=2,'ctx'=4,'tp'=4] {'fsdp','ctx'}, dimensions={0} | all-to-all | bytes 2621440 | tf_op jit(solution)/shard_map/all_to_all | solution.py:410
  260.2 33.9 %all_to_all.70 = bf16[8,160,512]{2,1,0:T(8,128)(2,1)} all-to-all(bf16[8,160,512]{2,1,0:T(8,128)(2,1)S(1)} %bitcast.178), channel_id=1, replica_groups=mesh['fsdp'=2,'ctx'=4,'tp'=4] {'fsdp','ctx'}, dimensions={0} | all-to-all | bytes 2621440 | tf_op jit(solution)/shard_map/all_to_all | solution.py:410
  297.3 4.2 copy.80
  301.4 6.6 reshape.267
  312.8 4.5 all-to-all-start.3
  317.3 70.7 %all-to-all-done.3 = bf16[8,256,768]{2,1,0:T(8,128)(2,1)} async-done(((bf16[8,256,768]{2,1,0:T(8,128)(2,1)}), bf16[8,256,768]{2,1,0:T(8,128)(2,1)}, u32[]{:S(2)}, u32[]{:S(2)}) %all-to-all-start.3) | async-done | bytes 3145760 | tf_op jit(solution)/shard_map/all_to_all | solution.py:389
  388.1 7.6 fusion.4
  395.7 6.3 multiply_reduce_fusion.3
  402.1 6.4 psum.58
  408.4 3.8 all-to-all-start.8
  412.3 6.4 all-to-all-done.8
  419.7 9.0 all_to_all.71
  432.3 6.7 convolution_convert_fusion
  439.1 49.1 %reduce-scatter.12.cloned.1.call-done = bf16[8,160,512]{2,1,0:T(8,128)(2,1)} async-done(((bf16[8,160,2048]{2,1,0:T(8,128)(2,1)}), bf16[8,160,512]{2,1,0:T(8,128)(2,1)}) %reduce-scatter.12.cloned.1.call-update) | async-done | bytes 1310736 | tf_op jit(solution)/shard_map/reduce_scatter | solution.py:415
  488.2 5.5 all-to-all-start.7
  495.0 31.0 %all-to-all-done.7 = bf16[8,160,512]{2,1,0:T(8,128)(2,1)} async-done(((bf16[8,160,512]{2,1,0:T(8,128)(2,1)}), bf16[8,160,512]{2,1,0:T(8,128)(2,1)}, u32[]{:S(2)}, u32[]{:S(2)}) %all-to-all-start.7) | async-done | bytes 1310752 | tf_op jit(solution)/shard_map/all_to_all | solution.py:418
  530.7 6.6 psum.59
  540.3 5.1 convolution_convert_fusion.1
  545.4 9.0 all-gather.21.cloned.1.call-done
  557.8 4.6 all-to-all-start.9
  563.7 8.1 all-to-all-done.9
  585.5 31.8 %psum.60 = f32[2,1024]{1,0:T(2,128)} all-reduce(f32[2,1024]{1,0:T(2,128)} %pad_maximum_fusion.11), channel_id=1, replica_groups=mesh['fsdp'=2,'ctx'=4,'tp'=4] {'ctx','tp'}, use_global_device_ids=true, to_apply=%region_24.25 | all-reduce | flops 2048 | bytes 16384 | tf_op jit(solution)/shard_map/psum | solution.py:540
  622.9 4.4 convolution_convert_fusion.2
  631.0 8.2 copy.87
  639.2 8.1 copy.85
  647.3 4.2 convolution_convert_fusion.9
  657.2 5.9 all-to-all-done.5
  663.1 4.5 all-to-all-start.11
  669.6 5.7 all_gather.43
  680.3 5.7 convolution_convert_fusion.6
  686.1 69.0 %all-to-all-done.11 = bf16[8,256,768]{2,1,0:T(8,128)(2,1)} async-done(((bf16[8,256,768]{2,1,0:T(8,128)(2,1)}), bf16[8,256,768]{2,1,0:T(8,128)(2,1)}, u32[]{:S(2)}, u32[]{:S(2)}) %all-to-all-start.11) | async-done | bytes 3145760 | tf_op jit(solution)/shard_map/all_to_all | solution.py:502
  767.0 28.5 %all-to-all-done.10 = bf16[8,256,384]{2,1,0:T(8,128)(2,1)S(1)} async-done(((bf16[8,256,384]{2,1,0:T(8,128)(2,1)}), bf16[8,256,384]{2,1,0:T(8,128)(2,1)S(1)}, u32[]{:S(2)}, u32[]{:S(2)}) %all-to-all-start.10) | async-done | bytes 1572896 | tf_op jit(solution)/shard_map/all_to_all | solution.py:555
  800.4 5.7 all-reduce
  808.1 14.2 %reduce-scatter.20.cloned.1.call-done = f32[256,8]{0,1:T(8,128)} async-done(((f32[2048,8]{0,1:T(8,128)}), f32[256,8]{0,1:T(8,128)}) %reduce-scatter.20.cloned.1.call-update) | async-done | bytes 8208 | tf_op jit(solution)/shard_map/reduce_scatter | solution.py:517
  823.6 5.9 reshape.265
  829.4 6.9 copy.105
  840.6 4.9 psum.63
  845.6 10.6 %all_gather.42 = f32[2,512]{1,0:T(2,128)S(1)} all-gather(f32[2,128]{1,0:T(2,128)S(1)} %psum.63), channel_id=1, replica_groups=mesh['fsdp'=2,'ctx'=4,'tp'=4] {'ctx'}, dimensions={1}, use_global_device_ids=true | all-gather | bytes 5120 | tf_op jit(solution)/shard_map/all_gather | solution.py:552
  858.1 54.2 %reduce-scatter.18.cloned.1.call-done = bf16[256,512]{1,0:T(8,128)(2,1)} async-done(((bf16[2048,512]{1,0:T(8,128)(2,1)}), bf16[256,512]{1,0:T(8,128)(2,1)}) %reduce-scatter.18.cloned.1.call-update) | async-done | bytes 262160 | tf_op jit(solution)/shard_map/reduce_scatter | solution.py:522
  915.3 14.3 %all-gather.23.cloned.1.call-done = bf16[256,2048]{1,0:T(8,128)(2,1)} async-done(((bf16[256,512]{1,0:T(8,128)(2,1)}), bf16[256,2048]{1,0:T(8,128)(2,1)}) %all-gather.23.cloned.1.call-update) | async-done | bytes 1048592 | tf_op jit(solution)/shard_map/all_gather | solution.py:581
  (292 shorter events, 127.8 us)
Async XLA Ops:
  7.2 58.1 %all-gather.11.cloned.1.call-start = ((), (), s32[]{:S(2)}) async-start(), calls=%async_computation.20 | async-start | bytes 2359296 | tf_op jit(solution)/shard_map/all_gather | solution.py:382
  10.0 28.8 %copy-start.6 = (bf16[1,256,2048]{2,1,0:T(8,128)(2,1)S(1)}, bf16[1,256,2048]{2,1,0:T(8,128)(2,1)}, u32[]{:S(2)}) copy-start(bf16[1,256,2048]{2,1,0:T(8,128)(2,1)} %param.11) | copy-start | bytes 3145732
  38.8 79.8 %all-gather.9.cloned.1.call-start = ((), (), s32[]{:S(2)}) async-start(), calls=%async_computation.19 | async-start | bytes 4456448 | tf_op jit(solution)/shard_map/all_gather | solution.py:431
  42.2 126.7 %all-gather.13.cloned.1.call-start = ((), (), s32[]{:S(2)}) async-start(), calls=%async_computation.21 | async-start | bytes 2359296 | tf_op jit(solution)/shard_map/all_gather | solution.py:393
  43.0 117.3 %copy-start.29 = (s32[1024]{0:T(1024)}, s32[1024]{0:T(1024)S(1)}, u32[]{:S(2)}) copy-start(s32[1024]{0:T(1024)S(1)} %add_select_fusion) | copy-start | bytes 12292
  43.7 112.0 %copy-start.59 = (f32[128]{0:T(128)}, f32[128]{0:T(128)S(1)}, u32[]{:S(2)}) copy-start(f32[128]{0:T(128)S(1)} %get-tuple-element.113) | copy-start | bytes 1540
  43.7 112.0 %copy-start.61 = (f32[128]{0:T(128)}, f32[128]{0:T(128)S(1)}, u32[]{:S(2)}) copy-start(f32[128]{0:T(128)S(1)} %get-tuple-element.114) | copy-start | bytes 1540
  43.8 112.5 %copy-start.7 = (f32[1024,64]{0,1:T(8,128)}, f32[1024,64]{0,1:T(8,128)S(1)}, u32[]{:S(2)}) copy-start(f32[1024,64]{0,1:T(8,128)S(1)} %broadcast_multiply_fusion) | copy-start | bytes 786436
  165.4 10.2 %all-to-all-start.1 = ((bf16[4,256,128]{1,2,0:T(8,128)(2,1)}), bf16[4,256,128]{1,2,0:T(8,128)(2,1)S(1)}, u32[]{:S(2)}, u32[]{:S(2)}) async-start(bf16[4,256,128]{1,2,0:T(8,128)(2,1)} %copy.79), calls=%async_computation.1 | async-start | bytes 524288 | tf_op jit(solution)/shard_map/all_to_all | solution.py:452
  168.8 41.5 %reduce-scatter.8.cloned.1.call-start = ((), (), s32[]{:S(2)}) async-start(), calls=%async_computation.22 | async-start | bytes 1310720 | tf_op jit(solution)/shard_map/reduce_scatter | solution.py:455
  179.1 209.0 %all-gather.15.cloned.1.call-start = ((), (), s32[]{:S(2)}) async-start(), calls=%async_computation.23 | async-start | bytes 6553600 | tf_op jit(solution)/shard_map/all_gather | solution.py:411
  179.2 128.8 %copy-start.55 = (f32[256]{0:T(256)}, f32[256]{0:T(256)S(1)}, u32[]{:S(2)}) copy-start(f32[256]{0:T(256)S(1)} %convert_element_type.177) | copy-start | bytes 3076
  179.4 239.3 %copy-start.41 = (s32[8,256]{1,0:T(8,128)}, s32[8,256]{1,0:T(8,128)S(1)}, u32[]{:S(2)}) copy-start(s32[8,256]{1,0:T(8,128)S(1)} %fusion.17) | copy-start | bytes 24580
  210.3 47.7 %copy-start.31 = (f32[2048,8]{0,1:T(8,128)}, f32[2048,8]{0,1:T(8,128)S(1)}, u32[]{:S(2)}) copy-start(f32[2048,8]{0,1:T(8,128)S(1)} %all_gather.36) | copy-start | bytes 196612
  222.8 189.4 %copy-start.34 = (f32[256,1]{0,1:T(1,128)}, f32[256,1]{0,1:T(1,128)S(1)}, u32[]{:S(2)}) copy-start(f32[256,1]{0,1:T(1,128)S(1)} %get-tuple-element.77) | copy-start | bytes 3076
  258.0 137.7 %all-gather.19.cloned.1.call-start = ((), (), s32[]{:S(2)}) async-start(), calls=%async_computation.26 | async-start | bytes 6553600 | tf_op jit(solution)/shard_map/all_gather | solution.py:411
  312.8 75.3 %all-to-all-start.3 = ((bf16[8,256,768]{2,1,0:T(8,128)(2,1)}), bf16[8,256,768]{2,1,0:T(8,128)(2,1)}, u32[]{:S(2)}, u32[]{:S(2)}) async-start(bf16[8,256,768]{2,1,0:T(8,128)(2,1)} %pad_maximum_fusion), calls=%async_computation.4 | async-start | bytes 6291456 | tf_op jit(solution)/shard_map/all_to_all | solution.py:389
  317.3 95.0 %copy-start.43 = (f32[256]{0:T(256)}, f32[256]{0:T(256)S(1)}, u32[]{:S(2)}) copy-start(f32[256]{0:T(256)S(1)} %fusion.59) | copy-start | bytes 3076
  317.3 94.9 %copy-start.50 = (f32[256]{0:T(256)}, f32[256]{0:T(256)S(1)}, u32[]{:S(2)}) copy-start(f32[256]{0:T(256)S(1)} %fusion.58) | copy-start | bytes 3076
  408.4 10.3 %all-to-all-start.8 = ((f32[8,1,160]{2,1,0:T(1,128)}), f32[8,1,160]{2,1,0:T(1,128)S(1)}, u32[]{:S(2)}, u32[]{:S(2)}) async-start(f32[8,1,160]{2,1,0:T(1,128)} %psum.58), calls=%async_computation.11 | async-start | bytes 16384 | tf_op jit(solution)/shard_map/all_to_all | solution.py:506
  412.2 75.9 %reduce-scatter.12.cloned.1.call-start = ((), (), s32[]{:S(2)}) async-start(), calls=%async_computation.27 | async-start | bytes 6553600 | tf_op jit(solution)/shard_map/reduce_scatter | solution.py:415
  432.3 6.8 copy-start.19
  432.3 6.8 copy-start.21
  488.2 37.8 %all-to-all-start.7 = ((bf16[8,160,512]{2,1,0:T(8,128)(2,1)}), bf16[8,160,512]{2,1,0:T(8,128)(2,1)}, u32[]{:S(2)}, u32[]{:S(2)}) async-start(bf16[8,160,512]{2,1,0:T(8,128)(2,1)} %reduce-scatter.12.cloned.1.call-done), calls=%async_computation.10 | async-start | bytes 2621440 | tf_op jit(solution)/shard_map/all_to_all | solution.py:418
  493.7 60.7 %all-gather.21.cloned.1.call-start = ((), (), s32[]{:S(2)}) async-start(), calls=%async_computation.28 | async-start | bytes 1310720 | tf_op jit(solution)/shard_map/all_gather | solution.py:520
  540.2 87.1 %reduce-scatter.10.cloned.1.call-start = ((), (), s32[]{:S(2)}) async-start(), calls=%async_computation.24 | async-start | bytes 6553600 | tf_op jit(solution)/shard_map/reduce_scatter | solution.py:415
  557.8 14.0 %all-to-all-start.9 = ((bf16[4,256,128]{2,1,0:T(8,128)(2,1)}), bf16[4,256,128]{2,1,0:T(8,128)(2,1)}, u32[]{:S(2)}, u32[]{:S(2)}) async-start(bf16[4,256,128]{2,1,0:T(8,128)(2,1)} %bitcast.187), calls=%async_computation.12 | async-start | bytes 524288 | tf_op jit(solution)/shard_map/all_to_all | solution.py:525
  562.4 106.9 %reduce-scatter.14.cloned.1.call-start = ((), (), s32[]{:S(2)}) async-start(), calls=%async_computation.29 | async-start | bytes 5242880 | tf_op jit(solution)/shard_map/reduce_scatter | solution.py:564
  627.3 35.7 %all-to-all-start.5 = ((bf16[8,160,512]{2,1,0:T(8,128)(2,1)}), bf16[8,160,512]{2,1,0:T(8,128)(2,1)S(1)}, u32[]{:S(2)}, u32[]{:S(2)}) async-start(bf16[8,160,512]{2,1,0:T(8,128)(2,1)} %reduce-scatter.10.cloned.1.call-done), calls=%async_computation.7 | async-start | bytes 2621440 | tf_op jit(solution)/shard_map/all_to_all | solution.py:418
  657.1 12.2 %copy-start.33 = (f32[8,256]{1,0:T(8,128)S(1)}, f32[8,256]{1,0:T(8,128)}, u32[]{:S(2)}) copy-start(f32[8,256]{1,0:T(8,128)} %get-tuple-element.68) | copy-start | bytes 24580
  657.1 12.2 %copy-start.36 = (f32[256,1]{0,1:T(1,128)S(1)}, f32[256,1]{0,1:T(1,128)}, u32[]{:S(2)}) copy-start(f32[256,1]{0,1:T(1,128)} %copy-done.34) | copy-start | bytes 3076
  657.1 12.2 %copy-start.45 = (f32[256]{0:T(256)S(1)}, f32[256]{0:T(256)}, u32[]{:S(2)}) copy-start(f32[256]{0:T(256)} %copy-done.43) | copy-start | bytes 3076
  657.1 12.2 %copy-start.52 = (f32[256]{0:T(256)S(1)}, f32[256]{0:T(256)}, u32[]{:S(2)}) copy-start(f32[256]{0:T(256)} %copy-done.50) | copy-start | bytes 3076
  657.1 12.2 %copy-start.58 = (f32[256]{0:T(256)S(1)}, f32[256]{0:T(256)}, u32[]{:S(2)}) copy-start(f32[256]{0:T(256)} %fusion.55) | copy-start | bytes 3076
  657.2 18.2 %copy-start.42 = (s32[8,256]{1,0:T(8,128)S(1)}, s32[8,256]{1,0:T(8,128)}, u32[]{:S(2)}) copy-start(s32[8,256]{1,0:T(8,128)} %copy-done.41) | copy-start | bytes 24580
  663.1 92.0 %all-to-all-start.11 = ((bf16[8,256,768]{2,1,0:T(8,128)(2,1)}), bf16[8,256,768]{2,1,0:T(8,128)(2,1)}, u32[]{:S(2)}, u32[]{:S(2)}) async-start(bf16[8,256,768]{2,1,0:T(8,128)(2,1)} %pad_maximum_fusion.1), calls=%async_computation.16 | async-start | bytes 6291456 | tf_op jit(solution)/shard_map/all_to_all | solution.py:502
  667.5 131.6 %reduce-scatter.16.cloned.1.call-start = ((), (), s32[]{:S(2)}) async-start(), calls=%async_computation.30 | async-start | bytes 1310720 | tf_op jit(solution)/shard_map/reduce_scatter | solution.py:565
  669.2 153.0 %reduce-scatter.20.cloned.1.call-start = ((), (), s32[]{:S(2)}) async-start(), calls=%async_computation.33 | async-start | bytes 73728 | tf_op jit(solution)/shard_map/reduce_scatter | solution.py:517
  675.3 165.3 %all-gather.17.cloned.1.call-start = ((), (), s32[]{:S(2)}) async-start(), calls=%async_computation.25 | async-start | bytes 1310720 | tf_op jit(solution)/shard_map/all_gather | solution.py:582
  676.7 235.6 %reduce-scatter.18.cloned.1.call-start = ((), (), s32[]{:S(2)}) async-start(), calls=%async_computation.32 | async-start | bytes 2359296 | tf_op jit(solution)/shard_map/reduce_scatter | solution.py:522
  755.1 40.4 %all-to-all-start.10 = ((bf16[8,256,384]{2,1,0:T(8,128)(2,1)}), bf16[8,256,384]{2,1,0:T(8,128)(2,1)S(1)}, u32[]{:S(2)}, u32[]{:S(2)}) async-start(bf16[8,256,384]{2,1,0:T(8,128)(2,1)} %bitcast.183), calls=%async_computation.15 | async-start | bytes 3145728 | tf_op jit(solution)/shard_map/all_to_all | solution.py:555
  758.7 170.9 %all-gather.23.cloned.1.call-start = ((), (), s32[]{:S(2)}) async-start(), calls=%async_computation.31 | async-start | bytes 1310720 | tf_op jit(solution)/shard_map/all_gather | solution.py:581
  798.7 7.3 copy-start.13
  798.8 7.3 copy-start.65
  798.8 7.3 copy-start.67
  798.8 23.5 %copy-start.54 = (bf16[256,8]{0,1:T(8,128)(2,1)S(1)}, bf16[256,8]{0,1:T(8,128)(2,1)}, u32[]{:S(2)}) copy-start(bf16[256,8]{0,1:T(8,128)(2,1)} %param.17) | copy-start | bytes 12292
  838.1 18.1 %copy-start.64 = (f32[256]{0:T(256)S(1)}, f32[256]{0:T(256)}, u32[]{:S(2)}) copy-start(f32[256]{0:T(256)} %copy-done.63) | copy-start | bytes 3076
  858.1 74.2 %copy-start.14 = (bf16[256,2048]{1,0:T(8,128)(2,1)S(1)}, bf16[256,2048]{1,0:T(8,128)(2,1)}, u32[]{:S(2)}) copy-start(bf16[256,2048]{1,0:T(8,128)(2,1)} %all-gather.17.cloned.1.call-done) | copy-start | bytes 3145732
  (49 other events, 122.3 us)
Sparse Core Ops, SparseCore 0:
  38.9 26.3 all-gather.10
  68.0 50.5 all-gather.8
  120.7 47.9 all-gather.12
  179.2 23.5 reduce-scatter.7
  258.1 37.8 all-gather.14
  297.5 40.4 all-gather.18
  439.2 48.8 reduce-scatter.11
  540.3 13.9 all-gather.20
  556.9 52.3 reduce-scatter.9
  627.4 41.7 reduce-scatter.13
  671.5 53.2 reduce-scatter.15
  728.5 93.7 reduce-scatter.19
  824.5 15.7 all-gather.16
  844.7 67.6 reduce-scatter.17
  913.8 15.6 all-gather.22

commit v2 on v1

--- a/solution.py
+++ b/solution.py
@@ -1,8 +1,11 @@
+import functools
 import math
 
 import jax
 import jax.numpy as jnp
 from jax import lax
+from jax.experimental import pallas as pl
+from jax.experimental.pallas import tpu as pltpu
 from jax.sharding import PartitionSpec as P
 
 HEAD_DIM = 128
@@ -335,6 +338,750 @@
         gate_up_share,
         down_share,
     )
+
+
+MESH = pl.DeviceIdType.MESH
+
+
+def remote(src, dst, send, recv, **where):
+    return pltpu.make_async_remote_copy(
+        src_ref=src, dst_ref=dst, send_sem=send, recv_sem=recv, device_id=where, device_id_type=MESH
+    )
+
+
+def greet(peers):
+    barrier = pltpu.get_barrier_semaphore()
+    for where in peers:
+        pl.semaphore_signal(barrier, inc=1, device_id=where, device_id_type=MESH)
+    pl.semaphore_wait(barrier, len(peers))
+
+
+def in_group(sizes, step):
+    _, n_ctx, n_tp = sizes
+    here = lax.axis_index("ctx") * n_tp + lax.axis_index("tp")
+    there = lax.rem(here + step, n_ctx * n_tp)
+    return {"ctx": there // n_tp, "tp": lax.rem(there, n_tp)}, there
+
+
+def rows_at(place, size):
+    return pl.ds(pl.multiple_of(place * size, size), size)
+
+
+def dot_f32(a, b, dims, precision=None):
+    return lax.dot_general(
+        a, b, (dims, ((), ())), precision=precision, preferred_element_type=jnp.float32
+    )
+
+
+def group_sum(sizes, own, parts, send, recv):
+    _, n_ctx, n_tp = sizes
+    others = n_ctx * n_tp - 1
+    here = lax.axis_index("ctx") * n_tp + lax.axis_index("tp")
+    copies = []
+    for step in range(1, others + 1):
+        where, _ = in_group(sizes, step)
+        copies.append(remote(own, parts.at[here], send.at[step - 1], recv.at[step - 1], **where))
+        copies[-1].start()
+    total = own[...]
+    for step in range(1, others + 1):
+        copies[step - 1].wait_recv()
+        _, there = in_group(sizes, others + 1 - step)
+        total = total + parts[there]
+    for copy in copies:
+        copy.wait_send()
+    return total
+
+
+def attend_kernel(
+    sizes,
+    scale,
+    own_rows,
+    weight,
+    gains,
+    cosine,
+    sine,
+    own_router,
+    normed,
+    head_weight,
+    query_proj,
+    key_proj,
+    query_rot,
+    key_rot,
+    value,
+    rms,
+    attended,
+    router,
+    own_attended,
+    own_sums,
+    sums,
+    w_send,
+    w_recv,
+    x_send,
+    x_recv,
+    n_send,
+    n_recv,
+    y_send,
+    y_recv,
+    c_send,
+    c_recv,
+    s_send,
+    s_recv,
+    a_send,
+    a_recv,
+    r_send,
+    r_recv,
+):
+    n_fsdp, n_ctx, n_tp = sizes
+    fsdp, ctx, tp = lax.axis_index("fsdp"), lax.axis_index("ctx"), lax.axis_index("tp")
+    block = own_rows.shape[0]
+    share = block // n_tp
+    half_dim = HEAD_DIM // 2
+    mate = tp + 1 - 2 * lax.rem(tp, 2)
+    over = lax.rem(tp + 2, n_tp)
+    over_mate = lax.rem(mate + 2, n_tp)
+    across = 1 - fsdp
+    places = n_fsdp * n_ctx
+    me = fsdp * n_ctx + ctx
+    greet(
+        [in_group(sizes, step)[0] for step in range(1, n_ctx * n_tp)]
+        + [
+            {"fsdp": across, "ctx": lax.rem(ctx + step, n_ctx)}
+            for step in range(n_ctx)
+        ]
+    )
+
+    copies = []
+
+    def go(*args, **where):
+        copy = remote(*args, **where)
+        copy.start()
+        copies.append(copy)
+        return copy
+
+    def back(step):
+        return lax.rem(ctx + n_ctx - step, n_ctx)
+
+    mine = rows_at(tp, share)
+    from_w, from_n, from_y, from_c, from_x = {}, {}, {}, {}, {}
+    for step in range(1, n_ctx):
+        there = lax.rem(ctx + step, n_ctx)
+        from_w[step] = go(
+            weight.at[there],
+            head_weight.at[fsdp * n_ctx + ctx],
+            w_send.at[step - 1],
+            w_recv.at[step - 1],
+            ctx=there,
+        )
+    from_x[0] = go(
+        weight.at[ctx],
+        head_weight.at[fsdp * n_ctx + ctx],
+        x_send.at[0],
+        x_recv.at[0],
+        fsdp=across,
+    )
+    for step in range(1, n_ctx):
+        there = lax.rem(ctx + step, n_ctx)
+        from_n[step] = go(
+            own_rows.at[mine], normed.at[ctx, mine], n_send.at[step - 1], n_recv.at[step - 1], ctx=there
+        )
+    from_r = []
+    for step in range(1, places):
+        there = later(sizes, step)
+        from_r.append(
+            go(
+                own_router,
+                router.at[me],
+                r_send.at[step - 1],
+                r_recv.at[step - 1],
+                **place_at(sizes, there),
+            )
+        )
+    router[me] = own_router[...]
+    head_weight[fsdp * n_ctx + ctx] = weight[ctx]
+    normed[ctx] = own_rows[...]
+    for step in range(1, n_ctx):
+        origin = back(step)
+        from_w[step].wait_recv()
+        piece = head_weight.at[fsdp * n_ctx + origin]
+        from_x[step] = go(piece, piece, x_send.at[step], x_recv.at[step], fsdp=across)
+        from_n[step].wait_recv()
+        piece = normed.at[origin, mine]
+        from_y[step] = go(piece, piece, y_send.at[step - 1], y_recv.at[step - 1], tp=over)
+        from_c[step, 0] = go(
+            piece, piece, c_send.at[step - 1, 0], c_recv.at[step - 1, 0], tp=mate
+        )
+    for step in range(1, n_ctx):
+        from_y[step].wait_recv()
+        piece = normed.at[back(step), rows_at(over, share)]
+        from_c[step, 1] = go(
+            piece, piece, c_send.at[step - 1, 1], c_recv.at[step - 1, 1], tp=mate
+        )
+    for step in range(n_ctx):
+        from_x[step].wait_recv()
+
+    width = head_weight.shape[0] * head_weight.shape[1]
+    line = lax.broadcasted_iota(jnp.int32, own_sums.shape, 0)
+    ones = jnp.ones((2 * n_ctx, HEAD_DIM), jnp.float32)
+    all_sums = jnp.zeros(own_sums.shape, jnp.float32)
+    for step in range(n_ctx):
+        if step:
+            from_c[step, 0].wait_recv()
+            from_c[step, 1].wait_recv()
+        origin = back(step)
+        here = rows_at(origin, block)
+        projected = dot_f32(
+            normed[origin], head_weight[...].reshape(width, 3 * HEAD_DIM), ((1,), (0,))
+        )
+        query, key = projected[:, :HEAD_DIM], projected[:, HEAD_DIM : 2 * HEAD_DIM]
+        query_proj[here] = query
+        key_proj[here] = key
+        value[here] = projected[:, 2 * HEAD_DIM :].astype(value.dtype)
+        query_sum = dot_f32(ones, query * query, ((1,), (1,)), highest)
+        key_sum = dot_f32(ones, key * key, ((1,), (1,)), highest)
+        all_sums = jnp.where(line == origin, query_sum, all_sums)
+        all_sums = jnp.where(line == origin + n_ctx, key_sum, all_sums)
+    own_sums[...] = all_sums
+    total = group_sum(sizes, own_sums, sums, s_send, s_recv)
+    inverse = lax.rsqrt(total / HQ + epsilon)
+    columns = inverse.T
+    rms[...] = columns
+    for place in range(n_ctx):
+        here = slice(place * block, (place + 1) * block)
+        cos_here, sin_here = cosine[here], sine[here]
+        for proj, rot, which in ((query_proj, query_rot, 0), (key_proj, key_rot, 1)):
+            scaled = proj[here] * columns[:, which * n_ctx + place][:, None] * gains[which]
+            turned = pltpu.roll(scaled, half_dim, 1)
+            rot[here] = (scaled * cos_here + turned * sin_here).astype(rot.dtype)
+    from_a = {}
+    for place in range(n_ctx):
+        here = slice(place * block, (place + 1) * block)
+        seen = slice(0, (place + 1) * block)
+        scores = dot_f32(query_rot[here], key_rot[seen], ((1,), (1,))) * scale
+        exponent = jnp.exp(scores - jnp.max(scores, axis=-1, keepdims=True))
+        probs = exponent / jnp.sum(exponent, axis=-1, keepdims=True)
+        mixed = dot_f32(probs.astype(value.dtype), value[seen], ((1,), (0,)))
+        own_attended[place] = mixed.astype(own_attended.dtype)
+        lanes = rows_at(ctx, HEAD_DIM)
+        from_a[place] = remote(
+            own_attended.at[place],
+            attended.at[:, lanes],
+            a_send.at[place],
+            a_recv.at[ctx],
+            ctx=place,
+        )
+
+        @pl.when(ctx != place)
+        def _():
+            from_a[place].start()
+
+        @pl.when(ctx == place)
+        def _():
+            attended[:, lanes] = own_attended[place]
+
+    for place in range(n_ctx):
+
+        @pl.when(ctx != place)
+        def _():
+            from_a[place].wait_send()
+            remote(
+                own_attended.at[place],
+                attended.at[:, rows_at(place, HEAD_DIM)],
+                a_send.at[place],
+                a_recv.at[place],
+                ctx=place,
+            ).wait_recv()
+
+    for copy in from_r:
+        copy.wait_recv()
+    for copy in copies:
+        copy.wait_send()
+
+
+def attend(sizes, own_rows, weight, gains, cosine, sine, router):
+    n_fsdp, n_ctx, n_tp = sizes
+    block, width = own_rows.shape
+    _, depth, columns = weight.shape
+    length = n_ctx * block
+    group = n_ctx * n_tp
+    bf16, f32 = jnp.bfloat16, jnp.float32
+    vmem = pl.BlockSpec(memory_space=pltpu.VMEM)
+    dma = pltpu.SemaphoreType.DMA
+    shape = jax.ShapeDtypeStruct
+    outs = (
+        shape((n_ctx, block, width), bf16),
+        shape((n_fsdp * n_ctx, depth, columns), bf16),
+        shape((length, HEAD_DIM), f32),
+        shape((length, HEAD_DIM), f32),
+        shape((length, HEAD_DIM), bf16),
+        shape((length, HEAD_DIM), bf16),
+        shape((length, HEAD_DIM), bf16),
+        shape((block, 2 * n_ctx), f32),
+        shape((block, n_ctx * HEAD_DIM), bf16),
+        shape((n_fsdp * n_ctx,) + router.shape, f32),
+    )
+    pairs = [
+        (n_ctx - 1,),
+        (n_ctx,),
+        (n_ctx - 1,),
+        (n_ctx - 1,),
+        (n_ctx - 1, 2),
+        (group - 1,),
+        (n_ctx,),
+        (n_fsdp * n_ctx - 1,),
+    ]
+    return pl.pallas_call(
+        functools.partial(attend_kernel, sizes, 1.0 / math.sqrt(HEAD_DIM)),
+        name="attend",
+        out_shape=outs,
+        in_specs=[vmem] * 6,
+        out_specs=(vmem,) * len(outs),
+        scratch_shapes=[
+            pltpu.VMEM((n_ctx, block, HEAD_DIM), bf16),
+            pltpu.VMEM((2 * n_ctx, block), f32),
+            pltpu.VMEM((group, 2 * n_ctx, block), f32),
+        ]
+        + [dma(size) for size in pairs for _ in range(2)],
+        compiler_params=pltpu.CompilerParams(collective_id=0, has_side_effects=True),
+        cost_estimate=pl.CostEstimate(
+            flops=70_000_000_000, bytes_accessed=20_000_000, transcendentals=1_000_000
+        ),
+    )(own_rows, weight, gains, cosine, sine, router)
+
+
+def signed_tables(offset, length):
+    cosine, sine = rotary_tables(offset, length)
+    half_dim = HEAD_DIM // 2
+    return cosine, jnp.concatenate([-sine[:, :half_dim], sine[:, half_dim:]], axis=1)
+
+
+def around(sizes):
+    n_fsdp, n_ctx, n_tp = sizes
+    me = lax.axis_index("fsdp") * n_ctx + lax.axis_index("ctx")
+    tp = lax.axis_index("tp")
+    mate = tp + 1 - 2 * lax.rem(tp, 2)
+    over = lax.rem(tp + 2, n_tp)
+    return me, tp, mate, over, lax.rem(mate + 2, n_tp)
+
+
+def place_at(sizes, place):
+    return {"fsdp": place // sizes[1], "ctx": lax.rem(place, sizes[1])}
+
+
+def later(sizes, step):
+    places = sizes[0] * sizes[1]
+    me = lax.axis_index("fsdp") * sizes[1] + lax.axis_index("ctx")
+    return lax.rem(me + step, places)
+
+
+def tp_sum(own, parts, send, recv, peers):
+    copies = [
+        remote(own, parts.at[i], send.at[i], recv.at[i], tp=peer) for i, peer in enumerate(peers)
+    ]
+    for copy in copies:
+        copy.start()
+    total = own[...]
+    for i, copy in enumerate(copies):
+        copy.wait_recv()
+        total = total + parts[i]
+    for copy in copies:
+        copy.wait_send()
+    return total
+
+
+def middle_kernel(
+    sizes,
+    attended,
+    out_all,
+    in_part,
+    router,
+    pick,
+    middle,
+    small,
+    chances,
+    normed,
+    rows,
+    gates,
+    c_out,
+    c_in,
+    y_out,
+    y_in,
+    own_small,
+    smalls,
+    rows_out,
+    gates_out,
+    m_send,
+    m_recv,
+    t_send,
+    t_recv,
+    z_send,
+    z_recv,
+    g_send,
+    g_recv,
+    y_send,
+    y_recv,
+    c_send,
+    c_recv,
+    d_send,
+    d_recv,
+):
+    bf16, f32 = jnp.bfloat16, jnp.float32
+    n_fsdp, n_ctx, n_tp = sizes
+    places = n_fsdp * n_ctx
+    me, tp, mate, over, over_mate = around(sizes)
+    quarter = in_part.shape[1]
+    width = quarter * n_tp
+    per = places // n_tp
+    greet(
+        [{"tp": peer} for peer in (mate, over, over_mate)]
+        + [place_at(sizes, later(sizes, step)) for step in range(1, places)]
+    )
+
+    def branch(which):
+        return dot_f32(attended[...], out_all[rows_at(which, quarter)], ((1,), (1,)))
+
+    to_mate = []
+    for i, which in enumerate((over_mate, mate)):
+        c_out[i] = branch(which).astype(bf16)
+        to_mate.append(remote(c_out.at[i], c_in.at[i], m_send.at[i], m_recv.at[i], tp=mate))
+        to_mate[i].start()
+    part = branch(over)
+    to_mate[0].wait_recv()
+    y_out[...] = (part + c_in[0].astype(f32)).astype(bf16)
+    to_over = remote(y_out, y_in, m_send.at[2], m_recv.at[2], tp=over)
+    to_over.start()
+    part = in_part[...] + branch(tp)
+    to_mate[1].wait_recv()
+    part = part + c_in[1].astype(f32)
+    to_over.wait_recv()
+    part = part + y_in[...].astype(f32)
+    for copy in (*to_mate, to_over):
+        copy.wait_send()
+    middle[...] = part
+
+    depth = quarter // per
+    raw = jnp.zeros((EXPERTS, part.shape[0]), f32)
+    for i in range(per):
+        raw = raw + dot_f32(
+            router[tp * per + i], part[:, i * depth : (i + 1) * depth], ((1,), (1,)), highest
+        )
+    own_small[:EXPERTS] = raw
+    own_small[EXPERTS:] = dot_f32(jnp.ones((8, quarter), f32), part * part, ((1,), (1,)), highest)
+    total = tp_sum(own_small, smalls, t_send, t_recv, (mate, over, over_mate))
+    inverse = lax.rsqrt(total[EXPERTS:] / width + epsilon)
+    small[:EXPERTS] = total[:EXPERTS]
+    small[EXPERTS:] = inverse
+    logits = total[:EXPERTS] * inverse[:1]
+    exponent = jnp.exp(logits - jnp.max(logits, axis=0, keepdims=True))
+    chances[...] = exponent / jnp.sum(exponent, axis=0, keepdims=True)
+    normed[...] = (part * inverse.T[:, :1]).astype(bf16)
+
+    lanes = rows_at(tp, quarter)
+    over_lanes = rows_at(over, quarter)
+
+    def own_row(step):
+        return remote(
+            rows_out.at[later(sizes, step)],
+            rows.at[me, :, lanes],
+            z_send.at[step],
+            z_recv.at[step],
+            **place_at(sizes, later(sizes, step)),
+        )
+
+    def own_gate(step):
+        return remote(
+            gates_out.at[later(sizes, step)],
+            gates.at[me],
+            g_send.at[step],
+            g_recv.at[step],
+            **place_at(sizes, later(sizes, step)),
+        )
+
+    def onward(step, which, send, recv, peer):
+        piece = rows.at[later(sizes, places - step), :, which]
+        return remote(piece, piece, send.at[step], recv.at[step], tp=peer)
+
+    def to_y(step):
+        return onward(step, lanes, y_send, y_recv, over)
+
+    def to_c(step):
+        return onward(step, lanes, c_send, c_recv, mate)
+
+    def to_d(step):
+        return onward(step, over_lanes, d_send, d_recv, mate)
+
+    def build(step, carry):
+        there = later(sizes, step)
+        rows_out[there] = dot_f32(pick[there], normed[...], ((1,), (0,))).astype(bf16)
+        chance = jnp.broadcast_to(chances[pl.ds(there, 1)], (8, chances.shape[1]))
+        gates_out[there, :, :CAP] = dot_f32(
+            chance, pick[there].astype(f32), ((1,), (1,)), highest
+        )
+
+        @pl.when(step < places)
+        def _():
+            own_row(step).start()
+            own_gate(step).start()
+
+        return carry
+
+    gates_out[...] = jnp.zeros_like(gates_out)
+    lax.fori_loop(1, places + 1, build, 0)
+    rows[me, :, lanes] = rows_out[me]
+    gates[me] = gates_out[me]
+    to_y(0).start()
+    to_c(0).start()
+
+    def pass_on(step, carry):
+        own_row(step).wait_recv()
+        to_y(step).start()
+        to_c(step).start()
+        to_y(step - 1).wait_recv()
+        to_d(step - 1).start()
+        return carry
+
+    lax.fori_loop(1, places, pass_on, 0)
+    to_y(places - 1).wait_recv()
+    to_d(places - 1).start()
+
+    def finish(step, carry):
+        to_c(step).wait_recv()
+        to_d(step).wait_recv()
+        to_c(step).wait_send()
+        to_d(step).wait_send()
+        to_y(step).wait_send()
+
+        @pl.when(step > 0)
+        def _():
+            own_row(step).wait_send()
+            own_gate(step).wait()
+
+        return carry
+
+    lax.fori_loop(0, places, finish, 0)
+
+
+def middle_stage(sizes, attended, out_all, in_part, router, pick):
+    n_fsdp, n_ctx, n_tp = sizes
+    places = n_fsdp * n_ctx
+    block, quarter = in_part.shape
+    bf16, f32 = jnp.bfloat16, jnp.float32
+    vmem = pl.BlockSpec(memory_space=pltpu.VMEM)
+    dma = pltpu.SemaphoreType.DMA
+    shape = jax.ShapeDtypeStruct
+    outs = (
+        shape((block, quarter), f32),
+        shape((EXPERTS + 8, block), f32),
+        shape((EXPERTS, block), f32),
+        shape((block, quarter), bf16),
+        shape((places, CAP, quarter * n_tp), bf16),
+        shape((places, 8, block), f32),
+    )
+    pairs = [3, 3, places, places, places, places, places]
+    return pl.pallas_call(
+        functools.partial(middle_kernel, sizes),
+        name="middle",
+        out_shape=outs,
+        in_specs=[vmem] * 5,
+        out_specs=(vmem,) * len(outs),
+        scratch_shapes=[
+            pltpu.VMEM((2, block, quarter), bf16),
+            pltpu.VMEM((2, block, quarter), bf16),
+            pltpu.VMEM((block, quarter), bf16),
+            pltpu.VMEM((block, quarter), bf16),
+            pltpu.VMEM((EXPERTS + 8, block), f32),
+            pltpu.VMEM((3, EXPERTS + 8, block), f32),
+            pltpu.VMEM((places, CAP, quarter), bf16),
+            pltpu.VMEM((places, 8, block), f32),
+        ]
+        + [dma((size,)) for size in pairs for _ in range(2)],
+        compiler_params=pltpu.CompilerParams(collective_id=1, has_side_effects=True),
+        cost_estimate=pl.CostEstimate(
+            flops=60_000_000_000, bytes_accessed=20_000_000, transcendentals=1_000_000
+        ),
+    )(attended, out_all, in_part, router, pick)
+
+
+def expert_kernel(
+    sizes,
+    rows,
+    up_rows,
+    weight,
+    gates,
+    back,
+    products,
+    act_low,
+    pre_grads,
+    returned,
+    keep,
+    c_out,
+    c_in,
+    y_out,
+    y_in,
+    z_out,
+    p_out,
+    c_send,
+    c_recv,
+    y_send,
+    y_recv,
+    z_send,
+    z_recv,
+    p_send,
+    p_recv,
+):
+    bf16, f32 = jnp.bfloat16, jnp.float32
+    n_fsdp, n_ctx, n_tp = sizes
+    places = n_fsdp * n_ctx
+    me, tp, mate, over, over_mate = around(sizes)
+    width = rows.shape[2]
+    quarter = width // n_tp
+    hidden = weight.shape[1] // 3
+    greet(
+        [{"tp": mate}, {"tp": over}]
+        + [place_at(sizes, later(sizes, step)) for step in range(1, places)]
+    )
+
+    def to_mate(i):
+        return remote(c_out.at[i], c_in.at[i], c_send.at[i], c_recv.at[i], tp=mate)
+
+    def to_over(i):
+        return remote(y_out.at[i], y_in.at[i], y_send.at[i], y_recv.at[i], tp=over)
+
+    def home(i):
+        there = later(sizes, i + 1)
+        return remote(
+            z_out.at[i], back.at[me], z_send.at[i], z_recv.at[i], **place_at(sizes, there)
+        )
+
+    def home_products(i):
+        there = later(sizes, i + 1)
+        return remote(
+            p_out.at[i], products.at[me], p_send.at[i], p_recv.at[i], **place_at(sizes, there)
+        )
+
+    def second(i):
+        to_mate(i).wait_recv()
+        y_out[i] = (keep[i, 0] + c_in[i, 0].astype(f32)).astype(bf16)
+        to_over(i).start()
+
+    def third(i):
+        to_over(i).wait_recv()
+        z_out[i] = (keep[i, 1] + c_in[i, 1].astype(f32) + y_in[i].astype(f32)).astype(bf16)
+
+        @pl.when(i < places - 1)
+        def _():
+            home(i).start()
+
+        @pl.when(i == places - 1)
+        def _():
+            back[me] = z_out[i]
+
+    p_out[...] = jnp.zeros_like(p_out)
+
+    def first(i, carry):
+        there = later(sizes, i + 1)
+        gate_up = dot_f32(rows[there], weight[:, : 2 * hidden], ((1,), (0,)))
+        act_grads = dot_f32(up_rows[there], weight[:, 2 * hidden :], ((1,), (0,)))
+        gate_part, up_part = gate_up[:, :hidden], gate_up[:, hidden:]
+        slot_gates = gates[there].T[:CAP, :1]
+        sigmoid = 1.0 / (1.0 + jnp.exp(-gate_part))
+        silu = gate_part * sigmoid
+        activated = silu * up_part
+        act = (activated * slot_gates).astype(bf16)
+        p_out[i, :, :CAP] = dot_f32(
+            jnp.ones((8, hidden), f32), activated * act_grads, ((1,), (1,)), highest
+        )
+        gated = act_grads * slot_gates
+        pre = jnp.concatenate(
+            [gated * up_part * sigmoid * (1.0 + gate_part * (1.0 - sigmoid)), gated * silu], axis=1
+        ).astype(bf16)
+        act_low[there] = act
+        pre_grads[there] = pre
+
+        def input_part(which):
+            return dot_f32(pre, weight[rows_at(which, quarter), : 2 * hidden], ((1,), (1,)))
+
+        c_out[i, 0] = input_part(over_mate).astype(bf16)
+        c_out[i, 1] = input_part(mate).astype(bf16)
+        to_mate(i).start()
+        keep[i, 0] = input_part(over)
+        keep[i, 1] = input_part(tp)
+
+        @pl.when(i < places - 1)
+        def _():
+            home_products(i).start()
+
+        @pl.when(i == places - 1)
+        def _():
+            products[me] = p_out[i]
+
+        @pl.when(i > 0)
+        def _():
+            second(i - 1)
+
+        returned[there] = dot_f32(act, weight[:, 2 * hidden :], ((1,), (1,))).astype(bf16)
+
+        @pl.when(i > 1)
+        def _():
+            third(i - 2)
+
+        return carry
+
+    lax.fori_loop(0, places, first, 0)
+    second(places - 1)
+    third(places - 2)
+    third(places - 1)
+
+    def finish(i, carry):
+        to_mate(i).wait_send()
+        to_over(i).wait_send()
+
+        @pl.when(i < places - 1)
+        def _():
+            home(i).wait()
+            home_products(i).wait()
+
+        return carry
+
+    lax.fori_loop(0, places, finish, 0)
+
+
+def expert_stage(sizes, rows, up_rows, weight, gates):
+    n_fsdp, n_ctx, n_tp = sizes
+    places, _, width = rows.shape
+    quarter = width // n_tp
+    hidden = weight.shape[1] // 3
+    bf16, f32 = jnp.bfloat16, jnp.float32
+    vmem = pl.BlockSpec(memory_space=pltpu.VMEM)
+    dma = pltpu.SemaphoreType.DMA
+    shape = jax.ShapeDtypeStruct
+    outs = (
+        shape((places, CAP, quarter), bf16),
+        shape(gates.shape, f32),
+        shape((places, CAP, hidden), bf16),
+        shape((places, CAP, 2 * hidden), bf16),
+        shape((places, CAP, width), bf16),
+    )
+    return pl.pallas_call(
+        functools.partial(expert_kernel, sizes),
+        name="expert",
+        out_shape=outs,
+        in_specs=[vmem] * 4,
+        out_specs=(vmem,) * len(outs),
+        scratch_shapes=[
+            pltpu.VMEM((places, 2, CAP, quarter), f32),
+            pltpu.VMEM((places, 2, CAP, quarter), bf16),
+            pltpu.VMEM((places, 2, CAP, quarter), bf16),
+            pltpu.VMEM((places, CAP, quarter), bf16),
+            pltpu.VMEM((places, CAP, quarter), bf16),
+            pltpu.VMEM((places, CAP, quarter), bf16),
+            pltpu.VMEM(gates.shape, f32),
+        ]
+        + [dma((places,)) for _ in range(8)],
+        compiler_params=pltpu.CompilerParams(collective_id=2, has_side_effects=True),
+        cost_estimate=pl.CostEstimate(
+            flops=50_000_000_000, bytes_accessed=30_000_000, transcendentals=1_000_000
+        ),
+    )(rows, up_rows, weight, gates)
 
 
 def attend_scores(query_rot, key_rot, scale, block):
@@ -378,9 +1125,6 @@
     qkv_raw = qkv_weight.reshape(depth, 3, n_ctx, HEAD_DIM).transpose(2, 0, 1, 3)
     qkv_raw = qkv_raw.reshape(n_ctx, depth, 3 * HEAD_DIM).astype(f32)
     qkv_scaled = (qkv_raw * attn_scale[None, :, None]).astype(bf16)
-    head_weight = lax.all_to_all(qkv_scaled, "ctx", 0, 0, tiled=True)
-    head_weight = lax.all_gather(head_weight, "fsdp", axis=0, tiled=True)
-    head_weight = head_weight.reshape(width, 3 * HEAD_DIM)
     gate_up_raw = gate_up_weight.transpose(2, 0, 1, 3).reshape(EXPERTS, depth, 2 * hidden)
     down_raw = down_weight.transpose(1, 0, 2)
     expert_send = jnp.concatenate(
@@ -388,12 +1132,9 @@
     )
     expert_weight = lax.all_to_all(expert_send, both, 0, 0, tiled=True)
     expert_weight = expert_weight.reshape(width, 3 * hidden)
-    gate_up_full = expert_weight[:, : 2 * hidden]
-    down_full = expert_weight[:, 2 * hidden :]
     out_all = lax.all_gather(out_weight, both, axis=0, tiled=True)
     router_f32 = router_weight.astype(f32)
-    router_all = lax.all_gather(router_f32 * mlp_scale[:, None], both, axis=0, tiled=True)
-    router_part = lax.dynamic_slice_in_dim(router_all, tp * quarter, quarter, axis=0)
+    router_own = (router_f32 * mlp_scale[:, None]).T
 
     routed = routes.reshape(block, TOPK)
     named = (routed[:, :, None] == jnp.arange(EXPERTS, dtype=jnp.int32)).astype(f32).sum(axis=1)
@@ -415,7 +1156,10 @@
         rows = lax.psum_scatter(
             rows.reshape(EXPERTS, CAP, width), "tp", scatter_dimension=2, tiled=True
         )
-        rows = lax.all_to_all(rows, both, 0, 0, tiled=True).reshape(EXPERTS * CAP, quarter)
+        return combine(lax.all_to_all(rows, both, 0, 0, tiled=True))
+
+    def combine(rows):
+        rows = rows.reshape(EXPERTS * CAP, quarter)
         return lax.dot_general(pick, rows, (((0,), (0,)), ((), ())), preferred_element_type=f32)
 
     upstream_part = own_quarter(cotangent.reshape(block, width))
@@ -426,71 +1170,48 @@
     first_rms = inv_rms(flat_in)
     in_part = own_quarter(flat_in)
     normed_own = (flat_in * first_rms).astype(bf16)
-    share = block // n_tp
-    normed_share = lax.dynamic_slice_in_dim(normed_own, tp * share, share, axis=0)
-    normed = lax.all_gather(normed_share, ("ctx", "tp"), axis=0, tiled=True)
-    projected = jnp.dot(normed, head_weight, preferred_element_type=f32)
-    query_proj = projected[:, :HEAD_DIM]
-    key_proj = projected[:, HEAD_DIM : 2 * HEAD_DIM]
-    value_heads = projected[:, 2 * HEAD_DIM :].astype(bf16)
-    sums = lax.psum(
-        jnp.stack([jnp.sum(query_proj * query_proj, axis=-1), jnp.sum(key_proj * key_proj, axis=-1)]),
-        ("ctx", "tp"),
-    )
-    query_rms = lax.rsqrt(sums[0] / HQ + epsilon)[:, None]
-    key_rms = lax.rsqrt(sums[1] / HQ + epsilon)[:, None]
     own_gains = lax.dynamic_slice_in_dim(qk_gains, ctx * HEAD_DIM, HEAD_DIM, axis=1).astype(f32)
+    own_gains = own_gains[:, None, :]
     query_gain, key_gain = own_gains[0], own_gains[1]
+    cosine, sine = signed_tables(0, length)
+    (
+        normed,
+        head_weight,
+        query_proj,
+        key_proj,
+        query_rot,
+        key_rot,
+        value_heads,
+        qk_rms,
+        attended,
+        router_blocks,
+    ) = attend(sizes, normed_own, qkv_scaled, own_gains, cosine, sine, router_own)
+    normed = normed.reshape(length, width)
+    head_weight = head_weight.reshape(width, 3 * HEAD_DIM)
+    query_rms = qk_rms[:, :n_ctx].T.reshape(length, 1)
+    key_rms = qk_rms[:, n_ctx:].T.reshape(length, 1)
     cosine, sine_table = rotary_tables(0, length)
-    query_rot = rotate(query_proj * query_rms * query_gain, cosine, sine_table).astype(bf16)
-    key_rot = rotate(key_proj * key_rms * key_gain, cosine, sine_table).astype(bf16)
     scores = attend_scores(query_rot, key_rot, scale, block)
     exponent = jnp.exp(scores - jnp.max(scores, axis=-1, keepdims=True))
     probs = exponent / jnp.sum(exponent, axis=-1, keepdims=True)
     probs_low = probs.astype(bf16)
-    attended = jnp.dot(probs_low, value_heads, preferred_element_type=f32).astype(bf16)
-    attended = lax.all_to_all(attended.reshape(n_ctx, block, HEAD_DIM), "ctx", 0, 0, tiled=True)
-    attended = attended.transpose(1, 0, 2).reshape(block, n_ctx * HEAD_DIM)
-    branch = jnp.einsum("th,dh->td", attended, out_all, preferred_element_type=f32)
-    branch = lax.psum_scatter(branch.astype(bf16), "tp", scatter_dimension=1, tiled=True)
-    middle = in_part + branch.astype(f32)
-
-    small = jnp.concatenate(
-        [
-            jnp.dot(middle, router_part, precision=highest),
-            jnp.sum(middle * middle, axis=-1, keepdims=True),
-        ],
-        axis=1,
-    )
-    small = lax.psum(small, "tp")
-    raw_logits = small[:, :EXPERTS]
-    second_rms = lax.rsqrt(small[:, EXPERTS:] / width + epsilon)
-    chances = jax.nn.softmax(raw_logits * second_rms, axis=-1)
-    normed_mlp = (middle * second_rms).astype(bf16)
-    rows = dispatch(normed_mlp)
-    slot_gates = jnp.sum(pick_f32 * chances.T[:, None, :], axis=-1)
-    slot_gates = lax.all_to_all(slot_gates, both, 0, 0, tiled=True).reshape(EXPERTS * CAP, 1)
-
-    gate_up = jnp.dot(rows, gate_up_full, preferred_element_type=f32)
-    gate_part, up_part = gate_up[:, :hidden], gate_up[:, hidden:]
-    sigmoid = jax.nn.sigmoid(gate_part)
-    silu = gate_part * sigmoid
-    activated = silu * up_part
-    act_low = (activated * slot_gates).astype(bf16)
-    act_grads = jnp.dot(up_rows, down_full, preferred_element_type=f32)
-    slot_products = jnp.sum(activated * act_grads, axis=-1)
-    gated = act_grads * slot_gates
-    pre_grads = jnp.concatenate(
-        [gated * up_part * sigmoid * (1.0 + gate_part * (1.0 - sigmoid)), gated * silu], axis=1
-    ).astype(bf16)
-    back_rows = lax.dot_general(
-        pre_grads, gate_up_full, (((1,), (1,)), ((), ())), preferred_element_type=f32
-    )
-    back_part = bring_back(back_rows.astype(bf16))
-    returned = lax.dot_general(
-        act_low, down_full, (((1,), (1,)), ((), ())), preferred_element_type=f32
-    )
-    output_part = (middle + bring_back(returned.astype(bf16))).astype(bf16)
+    middle, small, chances, normed_mlp, rows, slot_gates = middle_stage(
+        sizes, attended, out_all, in_part, router_blocks, pick.reshape(EXPERTS, CAP, block)
+    )
+    second_rms = small[EXPERTS][:, None]
+    chances = chances.T
+    per = places // n_tp
+    router_part = lax.dynamic_slice_in_dim(router_blocks, tp * per, per, axis=0)
+    router_part = router_part.transpose(0, 2, 1).reshape(quarter, EXPERTS)
+
+    back_rows, slot_products, act_low, pre_grads, returned = expert_stage(
+        sizes, rows, up_rows.reshape(places, CAP, width), expert_weight, slot_gates
+    )
+    rows = rows.reshape(EXPERTS * CAP, width)
+    act_low = act_low.reshape(EXPERTS * CAP, hidden)
+    pre_grads = pre_grads.reshape(EXPERTS * CAP, 2 * hidden)
+    back_part = combine(back_rows)
+    output_part = (middle + bring_back(returned)).astype(bf16)
     rows_in = (((0,), (0,)), ((), ()))
     expert_grads = jnp.concatenate(
         [
@@ -502,8 +1223,7 @@
     expert_grads = lax.all_to_all(
         expert_grads.reshape(EXPERTS, depth, 3 * hidden), both, 0, 0, tiled=True
     ).astype(f32)
-    slot_products = lax.psum(slot_products, "tp").reshape(EXPERTS, CAP)
-    slot_products = lax.all_to_all(slot_products, both, 0, 0, tiled=True)
+    slot_products = lax.psum(slot_products[:, 0, :CAP], "tp")
 
     chance_grads = jnp.sum(pick_f32 * slot_products[:, :, None], axis=1).T
     logit_grads = chances * (chance_grads - jnp.sum(chances * chance_grads, axis=-1, keepdims=True))

time: 952 us -> 779 us (0.82)
  Pallas kernels: 0 us -> 269 us
  waiting for transfers between devices: 444 us -> 230 us
  blocking collectives: 249 us -> 69.2 us
  matrix products: 77.7 us -> 50.1 us
  local copies, waits for them, and re-layouts: 66.8 us -> 48.6 us
    pallas_call x0 -> x3, Pallas kernels: none -> 269 us  [the longest x1 150 us: attend(): pl.pallas_call(functools.partial(attend_kernel, sizes, 1.0 / math.sqrt(HE...]
    all_to_all x4 -> x0, blocking collectives: 104 us -> none  [the longest x2 68.4 us: dispatch(): lax.all_to_all(rows.reshape(EXPERTS, CAP, quarter), both, 0, 0, tiled=True)]
    all_gather x2 -> x0, waiting for transfers between devices: 74.8 us -> none  [the longest x1 53.3 us: by_head(): normed = lax.all_gather(normed_share, ('ctx', 'tp'), axis=0, tiled=True)]
    all_to_all x1, waiting for transfers between devices: 70.7 us -> 0.01 us  [by_head(): expert_weight = lax.all_to_all(expert_send, both, 0, 0, tiled=True)]
    reduce_scatter x2 -> x1, waiting for transfers between devices: 49.1 us -> 0.01 us  [bring_back(): lax.psum_scatter(rows.reshape(EXPERTS, CAP, width), 'tp', scatter_dimensi...]
    psum x3 -> x1, blocking collectives: 48.9 us -> 5.92 us  [by_head(): slot_products = lax.psum(slot_products[:, 0, :CAP], 'tp')]
    all_to_all x4 -> x2, waiting for transfers between devices: 50 us -> 16.1 us  [the longest x1 15.1 us: bring_back(): return combine(lax.all_to_all(rows, both, 0, 0, tiled=True))]
    dot_general x10 -> x2, matrix products: 38.1 us -> 4.51 us  [combine(): lax.dot_general(pick, rows, (((0,), (0,)), ((), ())), preferred_element_t...]
  transfers between devices with their start and end apart: 23 -> 16, of which waited for: 16 -> 10; matrix products, arithmetic and copies ran while one was open for 16% -> 16% of each run, Pallas kernels for 0% -> 28%
where the time goes in v2:
time: 779 us; the launch traced here: 771 us
  Pallas kernels  269 us (35%)
  waiting for transfers between devices  230 us (30%)
  blocking collectives  69.2 us (9%)
  other arithmetic  57.9 us (7%)
  matrix products  50.1 us (6%)
  local copies, waits for them, and re-layouts  48.6 us (6%)
  starting transfers between devices  30.2 us (4%)
  between operations  15.4 us (2%)
    pallas_call x1, Pallas kernels, attend(): pl.pallas_call(functools.partial(attend_kernel, sizes, 1.0 / math.sqrt(HE...  150 us
    all_to_all x1, waiting for transfers between devices, by_head(): lax.all_to_all(expert_grads.reshape(EXPERTS, depth, 3 * hidden), both, 0,...  73.5 us
    pallas_call x1, Pallas kernels, middle_stage(): pl.pallas_call(functools.partial(middle_kernel, sizes), name='middle', ou...  62.6 us
    pallas_call x1, Pallas kernels, expert_stage(): pl.pallas_call(functools.partial(expert_kernel, sizes), name='expert', ou...  56.4 us
    reduce_scatter x1, waiting for transfers between devices, by_head(): lax.psum_scatter(grad_out.astype(bf16), both, scatter_dimension=0, tiled=...  36.3 us
    psum x1, blocking collectives, by_head(): lax.psum(jnp.stack([jnp.sum(query_scaled * query_proj, axis=-1), jnp.sum(...  30.3 us
    reduce_scatter x1, waiting for transfers between devices, by_head(): lax.psum_scatter(router_term, both, scatter_dimension=0, tiled=True)  27 us
    all_to_all x1, waiting for transfers between devices, by_head(): lax.all_to_all(qkv_grads.astype(bf16).reshape(places, depth, 3 * HEAD_DIM...  24.8 us
  transfers between devices with their start and end apart: 16, of which 10 were waited for; matrix products, arithmetic and copies ran while one was open for 16% of the time, Pallas kernels for 28%

profile of v2, /device:TPU:0, one launch (start us, length us, event | category | flops | bytes accessed | tf_op | source)
XLA Modules:
  0.0 770.7 jit_solution(14128939624683357876)
XLA Ops:
  10.0 2.5 convolution_convert_fusion.2
  12.5 7.3 all-to-all-start
  21.1 2.7 fusion.27
  24.0 4.2 convert_bitcast_fusion
  34.9 6.3 copy.78
  41.2 6.5 reshape.251
  51.2 2.9 multiply_convert_fusion.1
  60.6 4.9 all-to-all-start.1
  66.8 149.9 %attend.1 = (bf16[4,256,2048]{2,1,0:T(8,128)(2,1)}, bf16[8,256,384]{2,1,0:T(8,128)(2,1)}, f32[1024,128]{1,0:T(8,128)}, f32[1024,128]{1,0:T(8,128)}, bf16[1024,12...) custom-call(bf16[256,2048]{1,0:T(8,128)(2,1)} %fusion.5.own_rows, ...), custom_call_target="tpu_custom_call" | custom-call | flops 70000001024 | bytes 20000000 | tf_op jit(solution)/shard_map/attend/pallas_call | solution.py:632
  218.6 62.6 %middle.1 = (f32[256,512]{1,0:T(8,128)}, f32[16,256]{1,0:T(8,128)}, f32[8,256]{1,0:T(8,128)}, bf16[256,512]{1,0:T(8,128)(2,1)}, bf16[8,160,2048]{2,1,0:T(8,128)(2,1)}, /*index=5*/f32[8,8,256]{2,1,0:T(8,128)}) custom-call(bf16[256,512]{1,0:T(8,128)(2,1)} %get-tuple-element.31.attended, bf16[2048,512]{1,0:T(8,128)(2,1)} %all-gather.6.cloned.1.call-done.out_all, ...), custom_call_target="tpu_custom_call" | custom-call | flops 60000002048 | bytes 20000000 | tf_op jit(solution)/shard_map/middle/pallas_call | solution.py:880
  282.0 56.4 %expert.1 = (bf16[8,160,512]{2,1,0:T(8,128)(2,1)}, f32[8,8,256]{2,1,0:T(8,128)}, bf16[8,160,256]{2,1,0:T(8,128)(2,1)}, bf16[8,160,512]{2,1,0:T(8,128)(2,1)}, bf16[8,160,2048]{2,1,0:T(8,128)(2,1)}) custom-call(bf16[8,160,2048]{2,1,0:T(8,128)(2,1)} %get-tuple-element.34.rows, bf16[8,160,2048]{2,1,0:T(8,128)(2,1)} %all-gather.8.cloned.1.call-done.up_rows, ...), custom_call_target="tpu_custom_call" | custom-call | flops 49999998976 | bytes 30000000 | tf_op jit(solution)/shard_map/expert/pallas_call | solution.py:1064
  341.3 5.9 psum.42
  348.2 6.6 psum.43
  357.2 2.7 fusion.2
  359.9 13.4 %all-gather.12.cloned.1.call-done = bf16[256,2048]{1,0:T(8,128)(2,1)} async-done(((bf16[256,512]{1,0:T(8,128)(2,1)}), bf16[256,2048]{1,0:T(8,128)(2,1)}) %all-gather.12.cloned.1.call-update) | async-done | bytes 1048592 | tf_op jit(solution)/shard_map/all_gather | solution.py:1240
  373.3 2.6 fusion.19
  376.7 4.6 all-to-all-start.3
  381.3 3.2 fusion.1
  384.5 6.1 all-to-all-done.3
  390.6 4.3 fusion.15
  398.1 2.5 fusion.47
  400.9 2.6 multiply_reduce_fusion.3
  406.0 30.3 %psum.44 = f32[2,1024]{1,0:T(2,128)S(1)} all-reduce(f32[2,1024]{1,0:T(2,128)S(1)} %pad_maximum_fusion.7), channel_id=1, replica_groups=mesh['fsdp'=2,'ctx'=4,'tp'=4] {'ctx','tp'}, use_global_device_ids=true, to_apply=%region_13.14 | all-reduce | flops 2048 | bytes 16384 | tf_op jit(solution)/shard_map/psum | solution.py:1260
  437.4 5.9 convolution_convert_fusion
  444.2 6.2 convolution_convert_fusion.3
  450.4 3.6 all-to-all-start.4
  454.0 4.4 fusion.3
  458.4 6.4 bitcast_convert_fusion
  466.7 24.8 %all-to-all-done.4 = bf16[8,256,384]{2,1,0:T(8,128)(2,1)S(1)} async-done(((bf16[8,256,384]{2,1,0:T(8,128)(2,1)}), bf16[8,256,384]{2,1,0:T(8,128)(2,1)S(1)}, u32[]{:S(2)}, u32[]{:S(2)}) %all-to-all-start.4) | async-done | bytes 1572896 | tf_op jit(solution)/shard_map/all_to_all | solution.py:1275
  491.5 4.5 all-to-all-start.5
  497.8 5.7 all_gather.27
  509.7 73.5 %all-to-all-done.5 = bf16[8,256,768]{2,1,0:T(8,128)(2,1)} async-done(((bf16[8,256,768]{2,1,0:T(8,128)(2,1)}), bf16[8,256,768]{2,1,0:T(8,128)(2,1)}, u32[]{:S(2)}, u32[]{:S(2)}) %all-to-all-start.5) | async-done | bytes 3145760 | tf_op jit(solution)/shard_map/all_to_all | solution.py:1223
  583.2 5.1 convert_element_type.160
  588.3 4.3 all-to-all-start.2
  593.0 6.2 slice_multiply_fusion
  600.5 5.8 all-reduce
  608.4 15.1 %all-to-all-done.2 = bf16[8,160,512]{2,1,0:T(8,128)(2,1)} async-done(((bf16[8,160,512]{2,1,0:T(8,128)(2,1)}), bf16[8,160,512]{2,1,0:T(8,128)(2,1)}, u32[]{:S(2)}, u32[]{:S(2)}) %all-to-all-start.2) | async-done | bytes 1310752 | tf_op jit(solution)/shard_map/all_to_all | solution.py:1159
  623.4 2.6 fusion.18
  626.0 27.0 %reduce-scatter.14.cloned.1.call-done = f32[256,8]{0,1:T(8,128)} async-done(((f32[2048,8]{0,1:T(8,128)}), f32[256,8]{0,1:T(8,128)}) %reduce-scatter.14.cloned.1.call-update) | async-done | bytes 8208 | tf_op jit(solution)/shard_map/reduce_scatter | solution.py:1237
  654.4 4.9 psum.47
  659.3 9.9 %all_gather.26 = f32[2,512]{1,0:T(2,128)S(1)} all-gather(f32[2,128]{1,0:T(2,128)S(1)} %psum.47), channel_id=1, replica_groups=mesh['fsdp'=2,'ctx'=4,'tp'=4] {'ctx'}, dimensions={1}, use_global_device_ids=true | all-gather | bytes 5120 | tf_op jit(solution)/shard_map/all_gather | solution.py:1272
  671.1 5.9 reshape.249
  677.0 6.7 copy.106
  685.5 2.5 copy.91
  688.0 36.3 %reduce-scatter.12.cloned.1.call-done = bf16[256,512]{1,0:T(8,128)(2,1)} async-done(((bf16[2048,512]{1,0:T(8,128)(2,1)}), bf16[256,512]{1,0:T(8,128)(2,1)}) %reduce-scatter.12.cloned.1.call-update) | async-done | bytes 262160 | tf_op jit(solution)/shard_map/reduce_scatter | solution.py:1242
  727.2 14.5 %all-gather.14.cloned.1.call-done = bf16[256,2048]{1,0:T(8,128)(2,1)} async-done(((bf16[256,512]{1,0:T(8,128)(2,1)}), bf16[256,2048]{1,0:T(8,128)(2,1)}) %all-gather.14.cloned.1.call-update) | async-done | bytes 1048592 | tf_op jit(solution)/shard_map/all_gather | solution.py:1301
  741.7 2.8 bitcast_convert_fusion.1
  744.5 16.0 %all-gather.10.cloned.1.call-done = bf16[256,2048]{1,0:T(8,128)(2,1)} async-done(((bf16[256,512]{1,0:T(8,128)(2,1)}), bf16[256,2048]{1,0:T(8,128)(2,1)}) %all-gather.10.cloned.1.call-update) | async-done | bytes 1048592 | tf_op jit(solution)/shard_map/all_gather | solution.py:1302
  (173 shorter events, 63.6 us)
Async XLA Ops:
  7.2 12.6 %copy-start.13 = (bf16[256,3,512]{2,0,1:T(8,128)(2,1)S(1)}, bf16[256,3,512]{2,0,1:T(8,128)(2,1)}, u32[]{:S(2)}) copy-start(bf16[256,3,512]{2,0,1:T(8,128)(2,1)} %param.13) | copy-start | bytes 2359300
  7.2 211.4 %all-gather.6.cloned.1.call-start = ((), (), s32[]{:S(2)}) async-start(), calls=%async_computation.11 | async-start | bytes 2359296 | tf_op jit(solution)/shard_map/all_gather | solution.py:1135
  8.8 10.9 %copy-start.19 = (s32[8,256]{1,0:T(8,128)}, s32[8,256]{1,0:T(8,128)S(1)}, u32[]{:S(2)}) copy-start(s32[8,256]{1,0:T(8,128)S(1)} %fusion.20) | copy-start | bytes 24580
  12.5 48.1 %all-to-all-start = ((bf16[8,160,512]{2,1,0:T(8,128)(2,1)}), bf16[8,160,512]{2,1,0:T(8,128)(2,1)}, u32[]{:S(2)}, u32[]{:S(2)}) async-start(bf16[8,160,512]{2,1,0:T(8,128)(2,1)} %bitcast.11), calls=%async_computation | async-start | bytes 2621440 | tf_op jit(solution)/shard_map/all_to_all | solution.py:1151
  20.0 12.4 %copy-start.4 = (bf16[256,3,512]{0,2,1:T(8,128)(2,1)}, bf16[256,3,512]{0,2,1:T(8,128)(2,1)S(1)}, u32[]{:S(2)}) copy-start(bf16[256,3,512]{0,2,1:T(8,128)(2,1)S(1)} %copy.75) | copy-start | bytes 2359300
  29.2 3.2 copy-start.31
  29.2 3.2 copy-start.32
  32.4 24.8 %copy-start.27 = (f32[256]{0:T(256)}, f32[256]{0:T(256)S(1)}, u32[]{:S(2)}) copy-start(f32[256]{0:T(256)S(1)} %convert_element_type.134) | copy-start | bytes 3076
  32.5 24.2 %copy-start.23 = (f32[256]{0:T(256)}, f32[256]{0:T(256)S(1)}, u32[]{:S(2)}) copy-start(f32[256]{0:T(256)S(1)} %convert_element_type.139) | copy-start | bytes 3076
  41.2 9.8 %copy-start.3 = (bf16[1,256,2048]{2,1,0:T(8,128)(2,1)S(1)}, bf16[1,256,2048]{2,1,0:T(8,128)(2,1)}, u32[]{:S(2)}) copy-start(bf16[1,256,2048]{2,1,0:T(8,128)(2,1)} %param.11) | copy-start | bytes 3145732
  51.2 2.9 copy-start.7
  56.6 3.9 copy-start.25
  60.6 221.4 %all-to-all-start.1 = ((bf16[8,256,768]{2,1,0:T(8,128)(2,1)}), bf16[8,256,768]{2,1,0:T(8,128)(2,1)}, u32[]{:S(2)}, u32[]{:S(2)}) async-start(bf16[8,256,768]{2,1,0:T(8,128)(2,1)} %pad_maximum_fusion), calls=%async_computation.1 | async-start | bytes 6291456 | tf_op jit(solution)/shard_map/all_to_all | solution.py:1133
  65.5 216.5 %all-gather.8.cloned.1.call-start = ((), (), s32[]{:S(2)}) async-start(), calls=%async_computation.12 | async-start | bytes 6553600 | tf_op jit(solution)/shard_map/all_gather | solution.py:1152
  66.3 307.1 %all-gather.12.cloned.1.call-start = ((), (), s32[]{:S(2)}) async-start(), calls=%async_computation.15 | async-start | bytes 1310720 | tf_op jit(solution)/shard_map/all_gather | solution.py:1240
  216.9 64.3 %copy-start.6 = (f32[1,256,2048]{2,1,0:T(8,128)}, f32[1,256,2048]{2,1,0:T(8,128)S(1)}, u32[]{:S(2)}) copy-start(f32[1,256,2048]{2,1,0:T(8,128)S(1)} %convert_element_type.127) | copy-start | bytes 6291460
  282.0 56.4 %copy-start.20 = (s32[8,256]{1,0:T(8,128)S(1)}, s32[8,256]{1,0:T(8,128)}, u32[]{:S(2)}) copy-start(s32[8,256]{1,0:T(8,128)} %copy-done.19) | copy-start | bytes 24580
  338.3 9.1 %copy-start.18 = (f32[8,256]{1,0:T(8,128)S(1)}, f32[8,256]{1,0:T(8,128)}, u32[]{:S(2)}) copy-start(f32[8,256]{1,0:T(8,128)} %get-tuple-element.39) | copy-start | bytes 24580
  338.3 9.1 %copy-start.9 = (f32[256,512]{1,0:T(8,128)S(1)}, f32[256,512]{1,0:T(8,128)}, u32[]{:S(2)}) copy-start(f32[256,512]{1,0:T(8,128)} %get-tuple-element.33) | copy-start | bytes 1572868
  338.4 18.5 %copy-start.14 = (f32[256,8]{1,0:T(8,128)S(1)}, f32[256,8]{1,0:T(8,128)}, u32[]{:S(2)}) copy-start(f32[256,8]{1,0:T(8,128)} %get-tuple-element.41) | copy-start | bytes 24580
  340.3 16.8 %copy-start.30 = (f32[2,128]{1,0:T(2,128)S(1)}, f32[2,128]{1,0:T(2,128)}, u32[]{:S(2)}) copy-start(f32[2,128]{1,0:T(2,128)} %fusion.43) | copy-start | bytes 3076
  340.3 16.8 %copy-start.16 = (bf16[1024,128]{1,0:T(8,128)(2,1)S(1)}, bf16[1024,128]{1,0:T(8,128)(2,1)}, u32[]{:S(2)}) copy-start(bf16[1024,128]{1,0:T(8,128)(2,1)} %get-tuple-element.42) | copy-start | bytes 786436
  340.3 16.8 %copy-start.17 = (bf16[1024,128]{1,0:T(8,128)(2,1)S(1)}, bf16[1024,128]{1,0:T(8,128)(2,1)}, u32[]{:S(2)}) copy-start(bf16[1024,128]{1,0:T(8,128)(2,1)} %get-tuple-element.43) | copy-start | bytes 786436
  376.7 13.9 %all-to-all-start.3 = ((bf16[4,256,128]{2,1,0:T(8,128)(2,1)}), bf16[4,256,128]{2,1,0:T(8,128)(2,1)S(1)}, u32[]{:S(2)}, u32[]{:S(2)}) async-start(bf16[4,256,128]{2,1,0:T(8,128)(2,1)} %bitcast.154), calls=%async_computation.4 | async-start | bytes 524288 | tf_op jit(solution)/shard_map/all_to_all | solution.py:1245
  381.3 114.8 %reduce-scatter.8.cloned.1.call-start = ((), (), s32[]{:S(2)}) async-start(), calls=%async_computation.16 | async-start | bytes 5242880 | tf_op jit(solution)/shard_map/reduce_scatter | solution.py:1284
  390.6 4.3 copy-start
  390.6 4.3 copy-start.35
  398.1 2.8 copy-start.12
  400.8 2.8 copy-start.11
  443.3 145.0 %reduce-scatter.6.cloned.1.call-start = ((), (), s32[]{:S(2)}) async-start(), calls=%async_computation.13 | async-start | bytes 6553600 | tf_op jit(solution)/shard_map/reduce_scatter | solution.py:1156
  450.4 41.1 %all-to-all-start.4 = ((bf16[8,256,384]{2,1,0:T(8,128)(2,1)}), bf16[8,256,384]{2,1,0:T(8,128)(2,1)S(1)}, u32[]{:S(2)}, u32[]{:S(2)}) async-start(bf16[8,256,384]{2,1,0:T(8,128)(2,1)} %bitcast.165), calls=%async_computation.7 | async-start | bytes 3145728 | tf_op jit(solution)/shard_map/all_to_all | solution.py:1275
  454.0 4.4 copy-start.34
  466.7 36.9 %copy-start.8 = (bf16[256,2048]{1,0:T(8,128)(2,1)S(1)}, bf16[256,2048]{1,0:T(8,128)(2,1)}, u32[]{:S(2)}) copy-start(bf16[256,2048]{1,0:T(8,128)(2,1)} %all-gather.12.cloned.1.call-done) | copy-start | bytes 3145732
  466.7 36.9 %copy-start.15 = (bf16[256,512]{1,0:T(8,128)(2,1)S(1)}, bf16[256,512]{1,0:T(8,128)(2,1)}, u32[]{:S(2)}) copy-start(bf16[256,512]{1,0:T(8,128)(2,1)} %get-tuple-element.31.attended) | copy-start | bytes 786436
  491.5 91.7 %all-to-all-start.5 = ((bf16[8,256,768]{2,1,0:T(8,128)(2,1)}), bf16[8,256,768]{2,1,0:T(8,128)(2,1)}, u32[]{:S(2)}, u32[]{:S(2)}) async-start(bf16[8,256,768]{2,1,0:T(8,128)(2,1)} %pad_maximum_fusion.1), calls=%async_computation.8 | async-start | bytes 6291456 | tf_op jit(solution)/shard_map/all_to_all | solution.py:1223
  496.0 103.2 %reduce-scatter.10.cloned.1.call-start = ((), (), s32[]{:S(2)}) async-start(), calls=%async_computation.17 | async-start | bytes 1310720 | tf_op jit(solution)/shard_map/reduce_scatter | solution.py:1285
  496.6 156.5 %reduce-scatter.14.cloned.1.call-start = ((), (), s32[]{:S(2)}) async-start(), calls=%async_computation.20 | async-start | bytes 73728 | tf_op jit(solution)/shard_map/reduce_scatter | solution.py:1237
  503.6 220.8 %reduce-scatter.12.cloned.1.call-start = ((), (), s32[]{:S(2)}) async-start(), calls=%async_computation.19 | async-start | bytes 2359296 | tf_op jit(solution)/shard_map/reduce_scatter | solution.py:1242
  505.7 3.7 copy-start.5
  509.7 83.3 %copy-start.24 = (f32[256]{0:T(256)S(1)}, f32[256]{0:T(256)}, u32[]{:S(2)}) copy-start(f32[256]{0:T(256)} %copy-done.23) | copy-start | bytes 3076
  588.3 35.1 %all-to-all-start.2 = ((bf16[8,160,512]{2,1,0:T(8,128)(2,1)}), bf16[8,160,512]{2,1,0:T(8,128)(2,1)}, u32[]{:S(2)}, u32[]{:S(2)}) async-start(bf16[8,160,512]{2,1,0:T(8,128)(2,1)} %reduce-scatter.6.cloned.1.call-done), calls=%async_computation.3 | async-start | bytes 2621440 | tf_op jit(solution)/shard_map/all_to_all | solution.py:1159
  592.6 13.7 %copy-start.10 = (f32[256,512]{1,0:T(8,128)S(1)}, f32[256,512]{1,0:T(8,128)}, u32[]{:S(2)}) copy-start(f32[256,512]{1,0:T(8,128)} %get-tuple-element.91) | copy-start | bytes 1572868
  592.6 13.7 %copy-start.26 = (f32[256]{0:T(256)S(1)}, f32[256]{0:T(256)}, u32[]{:S(2)}) copy-start(f32[256]{0:T(256)} %copy-done.25) | copy-start | bytes 3076
  592.6 13.7 %copy-start.29 = (f32[256]{0:T(256)S(1)}, f32[256]{0:T(256)}, u32[]{:S(2)}) copy-start(f32[256]{0:T(256)} %get-tuple-element.113) | copy-start | bytes 3076
  592.6 149.1 %all-gather.14.cloned.1.call-start = ((), (), s32[]{:S(2)}) async-start(), calls=%async_computation.18 | async-start | bytes 1310720 | tf_op jit(solution)/shard_map/all_gather | solution.py:1301
  600.4 52.6 %copy-start.22 = (bf16[256,8]{0,1:T(8,128)(2,1)S(1)}, bf16[256,8]{0,1:T(8,128)(2,1)}, u32[]{:S(2)}) copy-start(bf16[256,8]{0,1:T(8,128)(2,1)} %param.17) | copy-start | bytes 12292
  600.5 68.8 %copy-start.28 = (f32[256]{0:T(256)S(1)}, f32[256]{0:T(256)}, u32[]{:S(2)}) copy-start(f32[256]{0:T(256)} %copy-done.27) | copy-start | bytes 3076
  608.3 152.2 %all-gather.10.cloned.1.call-start = ((), (), s32[]{:S(2)}) async-start(), calls=%async_computation.14 | async-start | bytes 1310720 | tf_op jit(solution)/shard_map/all_gather | solution.py:1302
  (4 other events, 6.1 us)
Sparse Core Ops, SparseCore 0:
  10.1 77.5 all-gather.5
  89.3 73.2 all-gather.7
  356.9 16.3 all-gather.11
  443.4 41.7 reduce-scatter.7
  487.7 51.3 reduce-scatter.5
  541.3 33.5 reduce-scatter.9
  578.6 74.3 reduce-scatter.13
  657.6 66.7 reduce-scatter.11
  726.0 15.7 all-gather.13
  743.8 16.7 all-gather.9

commit v3 on v2

--- a/solution.py
+++ b/solution.py
@@ -1084,11 +1084,495 @@
     )(rows, up_rows, weight, gates)
 
 
-def attend_scores(query_rot, key_rot, scale, block):
-    scores = jnp.einsum("qd,kd->qk", query_rot, key_rot, preferred_element_type=jnp.float32) * scale
-    length = scores.shape[0]
-    place = jnp.arange(length, dtype=jnp.int32) // block
-    return jnp.where(place[None, :] <= place[:, None], scores, -1e30)
+def back_kernel(
+    sizes,
+    scale,
+    back,
+    pick_t,
+    pick,
+    products,
+    middle,
+    small,
+    chances,
+    upstream,
+    router,
+    out_all,
+    query_rot,
+    key_rot,
+    value,
+    query_proj,
+    key_proj,
+    rms,
+    gains,
+    cosine,
+    sine,
+    middle_grad,
+    branch_grad,
+    logit_grads,
+    proj_grads,
+    gain_terms,
+    inners,
+    own_small,
+    smalls,
+    own_att,
+    att,
+    query_grad,
+    key_grad,
+    value_grad,
+    own_sums,
+    sums,
+    t_send,
+    t_recv,
+    b_send,
+    b_recv,
+    z_send,
+    z_recv,
+    s_send,
+    s_recv,
+):
+    bf16, f32 = jnp.bfloat16, jnp.float32
+    n_fsdp, n_ctx, n_tp = sizes
+    places = n_fsdp * n_ctx
+    me, tp, mate, over, over_mate = around(sizes)
+    ctx = lax.axis_index("ctx")
+    block, quarter = middle.shape
+    width = quarter * n_tp
+    per = places // n_tp
+    depth = quarter // per
+    half_dim = HEAD_DIM // 2
+    greet([in_group(sizes, step)[0] for step in range(1, n_ctx * n_tp)])
+
+    combined = dot_f32(
+        pick_t[...], back[...].reshape(EXPERTS * CAP, quarter), ((1,), (0,))
+    )
+    line = lax.broadcasted_iota(jnp.int32, (EXPERTS, block), 0)
+    chance_grads = jnp.zeros((EXPERTS, block), f32)
+    for expert in range(EXPERTS):
+        found = dot_f32(
+            products[expert][:, :CAP], pick[expert].astype(f32), ((1,), (0,)), highest
+        )
+        chance_grads = jnp.where(line == expert, found, chance_grads)
+    own_small[:EXPERTS] = chance_grads
+    own_small[EXPERTS:] = dot_f32(
+        jnp.ones((8, quarter), f32), combined * middle[...], ((1,), (1,)), highest
+    )
+    total = tp_sum(own_small, smalls, t_send, t_recv, (mate, over, over_mate))
+    chance = chances[...]
+    chance_grads = total[:EXPERTS]
+    logits = chance * (chance_grads - jnp.sum(chance * chance_grads, axis=0, keepdims=True))
+    logit_grads[...] = logits
+    inner = total[EXPERTS:] + jnp.sum(logits * small[:EXPERTS], axis=0, keepdims=True)
+    inner = inner.T[:, :1]
+    inverse = small[EXPERTS:].T[:, :1]
+    for i in range(per):
+        lanes = slice(i * depth, (i + 1) * depth)
+        scaled = combined[:, lanes] + dot_f32(
+            logits, router[tp * per + i], ((0,), (0,)), highest
+        )
+        middle_grad[:, lanes] = (
+            upstream[:, lanes].astype(f32)
+            + inverse * scaled
+            - middle[:, lanes] * (inverse * inverse * inverse / width * inner)
+        )
+    mine, theirs = rows_at(tp, quarter), rows_at(over, quarter)
+    branch_grad[:, mine] = middle_grad[...].astype(bf16)
+    to_mate = remote(
+        branch_grad.at[:, mine], branch_grad.at[:, mine], b_send.at[0], b_recv.at[0], tp=mate
+    )
+    to_over = remote(
+        branch_grad.at[:, mine], branch_grad.at[:, mine], b_send.at[1], b_recv.at[1], tp=over
+    )
+    onward = remote(
+        branch_grad.at[:, theirs], branch_grad.at[:, theirs], b_send.at[2], b_recv.at[2], tp=mate
+    )
+    to_over.start()
+    to_mate.start()
+
+    def from_quarter(which):
+        return dot_f32(
+            branch_grad[:, rows_at(which, quarter)],
+            out_all[rows_at(which, quarter)],
+            ((1,), (0,)),
+        )
+
+    grad = from_quarter(tp)
+    to_mate.wait_recv()
+    grad = grad + from_quarter(mate)
+    to_over.wait_recv()
+    onward.start()
+    grad = grad + from_quarter(over)
+    onward.wait_recv()
+    grad = grad + from_quarter(over_mate)
+    for copy in (to_mate, to_over, onward):
+        copy.wait_send()
+    to_head = {}
+    for place in range(n_ctx):
+        own_att[place] = grad[:, place * HEAD_DIM : (place + 1) * HEAD_DIM].astype(bf16)
+        to_head[place] = remote(
+            own_att.at[place], att.at[ctx], z_send.at[place], z_recv.at[ctx], ctx=place
+        )
+
+        @pl.when(ctx != place)
+        def _():
+            to_head[place].start()
+
+        @pl.when(ctx == place)
+        def _():
+            att[ctx] = own_att[place]
+
+    key_grad[...] = jnp.zeros_like(key_grad)
+    value_grad[...] = jnp.zeros_like(value_grad)
+    for place in range(n_ctx):
+        here = slice(place * block, (place + 1) * block)
+        seen = slice(0, (place + 1) * block)
+        query = query_rot[here]
+        scores = dot_f32(query, key_rot[seen], ((1,), (1,))) * scale
+        exponent = jnp.exp(scores - jnp.max(scores, axis=-1, keepdims=True))
+        probs = exponent / jnp.sum(exponent, axis=-1, keepdims=True)
+
+        @pl.when(ctx != place)
+        def _():
+            remote(
+                own_att.at[place], att.at[place], z_send.at[place], z_recv.at[place], ctx=place
+            ).wait_recv()
+
+        grad = att[place]
+        prob_grads = dot_f32(grad, value[seen], ((1,), (1,)))
+        score_grads = (
+            probs * (prob_grads - jnp.sum(probs * prob_grads, axis=-1, keepdims=True))
+        ).astype(bf16)
+        query_grad[here] = dot_f32(score_grads, key_rot[seen], ((1,), (0,))) * scale
+        key_grad[seen] += dot_f32(score_grads, query, ((0,), (0,))) * scale
+        value_grad[seen] += dot_f32(probs.astype(bf16), grad, ((0,), (0,)))
+    line = lax.broadcasted_iota(jnp.int32, own_sums.shape, 0)
+    ones = jnp.ones((own_sums.shape[0], HEAD_DIM), f32)
+    all_sums = jnp.zeros(own_sums.shape, f32)
+    terms = [jnp.zeros((1, HEAD_DIM), f32), jnp.zeros((1, HEAD_DIM), f32)]
+    for place in range(n_ctx):
+        here = slice(place * block, (place + 1) * block)
+        for which, grads, proj in ((0, query_grad, query_proj), (1, key_grad, key_proj)):
+            turned = pltpu.roll(grads[here], half_dim, 1)
+            norm_grad = grads[here] * cosine[here] - turned * sine[here]
+            column = rms[:, which * n_ctx + place][:, None]
+            terms[which] = terms[which] + jnp.sum(
+                norm_grad * proj[here] * column, axis=0, keepdims=True
+            )
+            norm_grad = norm_grad * gains[which]
+            grads[here] = norm_grad
+            found = dot_f32(ones, norm_grad * proj[here], ((1,), (1,)), highest)
+            all_sums = jnp.where(line == which * n_ctx + place, found, all_sums)
+        low = value_grad[here].astype(bf16)
+        proj_grads[here, 2 * HEAD_DIM :] = low
+        found = dot_f32(
+            ones, low.astype(f32) * value[here].astype(f32), ((1,), (1,)), highest
+        )
+        all_sums = jnp.where(line == 2 * n_ctx + place, found, all_sums)
+    gain_terms[0] = terms[0]
+    gain_terms[1] = terms[1]
+    own_sums[...] = all_sums
+    total = group_sum(sizes, own_sums, sums, s_send, s_recv)
+    columns = total.T
+    inners[...] = columns
+    for place in range(n_ctx):
+        here = slice(place * block, (place + 1) * block)
+        for which, grads, proj in ((0, query_grad, query_proj), (1, key_grad, key_proj)):
+            at = which * n_ctx + place
+            column = rms[:, at][:, None]
+            pre = column * grads[here] - proj[here] * (
+                column * column * column / HQ * columns[:, at][:, None]
+            )
+            proj_grads[here, which * HEAD_DIM : (which + 1) * HEAD_DIM] = pre.astype(bf16)
+    for place in range(n_ctx):
+
+        @pl.when(ctx != place)
+        def _():
+            to_head[place].wait_send()
+
+
+def back_stage(
+    sizes,
+    back,
+    pick_t,
+    pick,
+    products,
+    middle,
+    small,
+    chances,
+    upstream,
+    router,
+    out_all,
+    query_rot,
+    key_rot,
+    value,
+    query_proj,
+    key_proj,
+    rms,
+    gains,
+    cosine,
+    sine,
+):
+    n_fsdp, n_ctx, n_tp = sizes
+    block, quarter = middle.shape
+    length = n_ctx * block
+    group = n_ctx * n_tp
+    lines = 4 * n_ctx
+    bf16, f32 = jnp.bfloat16, jnp.float32
+    vmem = pl.BlockSpec(memory_space=pltpu.VMEM)
+    dma = pltpu.SemaphoreType.DMA
+    shape = jax.ShapeDtypeStruct
+    outs = (
+        shape((block, quarter), f32),
+        shape((block, quarter * n_tp), bf16),
+        shape((EXPERTS, block), f32),
+        shape((length, 3 * HEAD_DIM), bf16),
+        shape((2, 1, HEAD_DIM), f32),
+        shape((block, lines), f32),
+    )
+    return pl.pallas_call(
+        functools.partial(back_kernel, sizes, 1.0 / math.sqrt(HEAD_DIM)),
+        name="back",
+        out_shape=outs,
+        in_specs=[vmem] * 19,
+        out_specs=(vmem,) * len(outs),
+        scratch_shapes=[
+            pltpu.VMEM((EXPERTS + 8, block), f32),
+            pltpu.VMEM((3, EXPERTS + 8, block), f32),
+            pltpu.VMEM((n_ctx, block, HEAD_DIM), bf16),
+            pltpu.VMEM((n_ctx, block, HEAD_DIM), bf16),
+            pltpu.VMEM((length, HEAD_DIM), f32),
+            pltpu.VMEM((length, HEAD_DIM), f32),
+            pltpu.VMEM((length, HEAD_DIM), f32),
+            pltpu.VMEM((lines, block), f32),
+            pltpu.VMEM((group, lines, block), f32),
+        ]
+        + [dma((size,)) for size in (3, 3, n_ctx, group - 1) for _ in range(2)],
+        compiler_params=pltpu.CompilerParams(collective_id=3, has_side_effects=True),
+        cost_estimate=pl.CostEstimate(
+            flops=60_000_000_000, bytes_accessed=20_000_000, transcendentals=1_000_000
+        ),
+    )(
+        back,
+        pick_t,
+        pick,
+        products,
+        middle,
+        small,
+        chances,
+        upstream,
+        router,
+        out_all,
+        query_rot,
+        key_rot,
+        value,
+        query_proj,
+        key_proj,
+        rms,
+        gains,
+        cosine,
+        sine,
+    )
+
+
+def final_kernel(
+    sizes,
+    proj_grads,
+    head_weight,
+    normed,
+    in_part,
+    middle_grad,
+    columns,
+    grad_inputs,
+    qkv_grads,
+    keep,
+    c_out,
+    c_in,
+    y_out,
+    y_in,
+    z_out,
+    z_in,
+    x_out,
+    x_in,
+    h_out,
+    c_send,
+    c_recv,
+    y_send,
+    y_recv,
+    z_send,
+    z_recv,
+    x_send,
+    x_recv,
+    h_send,
+    h_recv,
+    b_send,
+    b_recv,
+):
+    bf16, f32 = jnp.bfloat16, jnp.float32
+    n_fsdp, n_ctx, n_tp = sizes
+    me, tp, mate, over, over_mate = around(sizes)
+    fsdp, ctx = lax.axis_index("fsdp"), lax.axis_index("ctx")
+    across = 1 - fsdp
+    block, quarter = in_part.shape
+    width = quarter * n_tp
+    depth = qkv_grads.shape[1]
+    greet(
+        [{"tp": mate}, {"tp": over}, {"fsdp": across}]
+        + [{"ctx": lax.rem(ctx + step, n_ctx)} for step in range(1, n_ctx)]
+    )
+
+    def ahead(i):
+        return lax.rem(ctx + i + 1, n_ctx)
+
+    def to_mate(i):
+        return remote(c_out.at[i], c_in.at[i], c_send.at[i], c_recv.at[i], tp=mate)
+
+    def to_over(i):
+        return remote(y_out.at[i], y_in.at[i], y_send.at[i], y_recv.at[i], tp=over)
+
+    def home(i):
+        return remote(z_out.at[i], z_in.at[i], z_send.at[i], z_recv.at[i], ctx=ahead(i))
+
+    def to_across(i):
+        return remote(x_out.at[i], x_in.at[i], x_send.at[i], x_recv.at[i], fsdp=across)
+
+    def to_owner(i):
+        return remote(h_out.at[i], qkv_grads.at[ctx], h_send.at[i], h_recv.at[i], ctx=ahead(i))
+
+    def first(i, carry):
+        grads = proj_grads[rows_at(ahead(i), block)]
+
+        def part(which):
+            return dot_f32(grads, head_weight[rows_at(which, quarter)], ((1,), (1,)))
+
+        c_out[i, 0] = part(over_mate).astype(bf16)
+        c_out[i, 1] = part(mate).astype(bf16)
+        to_mate(i).start()
+        keep[i, 0] = part(over)
+        keep[i, 1] = part(tp)
+        return carry
+
+    def weight_part(side, i):
+        lanes = rows_at(side * n_ctx + ahead(i), depth)
+        total = jnp.zeros((depth, 3 * HEAD_DIM), f32)
+        for place in range(n_ctx):
+            total = total + dot_f32(
+                normed[place, :, lanes],
+                proj_grads[place * block : (place + 1) * block],
+                ((0,), (0,)),
+            )
+        return total
+
+    def second(i, carry):
+        to_mate(i).wait_recv()
+        y_out[i] = (keep[i, 0] + c_in[i, 0].astype(f32)).astype(bf16)
+        to_over(i).start()
+        x_out[i] = weight_part(across, i).astype(bf16)
+        to_across(i).start()
+        return carry
+
+    def third(i, carry):
+        to_over(i).wait_recv()
+        total = keep[i, 1] + c_in[i, 1].astype(f32) + y_in[i].astype(f32)
+        keep[i, 1] = total
+        z_out[i] = total.astype(bf16)
+
+        @pl.when(i < n_ctx - 1)
+        def _():
+            home(i).start()
+
+        own = weight_part(fsdp, i)
+        to_across(i).wait_recv()
+        h_out[i] = (own + x_in[i].astype(f32)).astype(bf16)
+
+        @pl.when(i < n_ctx - 1)
+        def _():
+            to_owner(i).start()
+
+        @pl.when(i == n_ctx - 1)
+        def _():
+            qkv_grads[ctx] = h_out[i]
+
+        return carry
+
+    lax.fori_loop(0, n_ctx, first, 0)
+    lax.fori_loop(0, n_ctx, second, 0)
+    lax.fori_loop(0, n_ctx, third, 0)
+    total = keep[n_ctx - 1, 1]
+    for i in range(n_ctx - 1):
+        home(i).wait_recv()
+        total = total + z_in[i].astype(f32)
+    first_rms, inner = columns[:, :1], columns[:, 1:2]
+    grad = middle_grad[...] + first_rms * total - in_part[...] * inner
+    mine, theirs = rows_at(tp, quarter), rows_at(over, quarter)
+    grad_inputs[:, mine] = grad.astype(bf16)
+    far = remote(
+        grad_inputs.at[:, mine], grad_inputs.at[:, mine], b_send.at[0], b_recv.at[0], tp=over
+    )
+    near = remote(
+        grad_inputs.at[:, mine], grad_inputs.at[:, mine], b_send.at[1], b_recv.at[1], tp=mate
+    )
+    onward = remote(
+        grad_inputs.at[:, theirs], grad_inputs.at[:, theirs], b_send.at[2], b_recv.at[2], tp=mate
+    )
+    far.start()
+    near.start()
+
+    def finish(i, carry):
+        to_mate(i).wait_send()
+        to_over(i).wait_send()
+        to_across(i).wait_send()
+
+        @pl.when(i < n_ctx - 1)
+        def _():
+            home(i).wait_send()
+            to_owner(i).wait()
+
+        return carry
+
+    lax.fori_loop(0, n_ctx, finish, 0)
+    far.wait_recv()
+    onward.start()
+    near.wait()
+    onward.wait()
+    far.wait_send()
+
+
+def final_stage(sizes, proj_grads, head_weight, normed, in_part, middle_grad, columns):
+    n_fsdp, n_ctx, n_tp = sizes
+    block, quarter = in_part.shape
+    width = quarter * n_tp
+    depth = width // (n_fsdp * n_ctx)
+    bf16, f32 = jnp.bfloat16, jnp.float32
+    vmem = pl.BlockSpec(memory_space=pltpu.VMEM)
+    dma = pltpu.SemaphoreType.DMA
+    shape = jax.ShapeDtypeStruct
+    outs = (
+        shape((block, width), bf16),
+        shape((n_ctx, depth, 3 * HEAD_DIM), bf16),
+    )
+    return pl.pallas_call(
+        functools.partial(final_kernel, sizes),
+        name="final",
+        out_shape=outs,
+        in_specs=[vmem] * 6,
+        out_specs=(vmem,) * len(outs),
+        scratch_shapes=[
+            pltpu.VMEM((n_ctx, 2, block, quarter), f32),
+            pltpu.VMEM((n_ctx, 2, block, quarter), bf16),
+            pltpu.VMEM((n_ctx, 2, block, quarter), bf16),
+            pltpu.VMEM((n_ctx, block, quarter), bf16),
+            pltpu.VMEM((n_ctx, block, quarter), bf16),
+            pltpu.VMEM((n_ctx, block, quarter), bf16),
+            pltpu.VMEM((n_ctx, block, quarter), bf16),
+            pltpu.VMEM((n_ctx, depth, 3 * HEAD_DIM), bf16),
+            pltpu.VMEM((n_ctx, depth, 3 * HEAD_DIM), bf16),
+            pltpu.VMEM((n_ctx, depth, 3 * HEAD_DIM), bf16),
+        ]
+        + [dma((size,)) for size in (n_ctx,) * 5 + (3,) for _ in range(2)],
+        compiler_params=pltpu.CompilerParams(collective_id=4, has_side_effects=True),
+        cost_estimate=pl.CostEstimate(
+            flops=60_000_000_000, bytes_accessed=20_000_000, transcendentals=1_000_000
+        ),
+    )(proj_grads, head_weight, normed, in_part, middle_grad, columns)
 
 
 def by_head(
@@ -1114,7 +1598,6 @@
     quarter = width // n_tp
     length = n_ctx * block
     hidden = gate_up_weight.shape[3]
-    scale = 1.0 / math.sqrt(HEAD_DIM)
     ctx, tp = lax.axis_index("ctx"), lax.axis_index("tp")
 
     def own_quarter(values):
@@ -1143,8 +1626,9 @@
     earlier = jnp.dot(before, named.astype(bf16), preferred_element_type=f32).astype(jnp.int32)
     slot_of = jnp.where(named > 0, earlier, -1)
     picks = slot_of.T[:, None, :] == jnp.arange(CAP, dtype=jnp.int32)[None, :, None]
-    pick_f32 = picks.astype(f32)
     pick = picks.astype(bf16).reshape(EXPERTS * CAP, block)
+    pick_t = (slot_of[:, :, None] == jnp.arange(CAP, dtype=jnp.int32)).astype(bf16)
+    pick_t = pick_t.reshape(block, EXPERTS * CAP)
 
     def dispatch(part):
         rows = jnp.dot(pick, part, preferred_element_type=f32).astype(bf16)
@@ -1164,7 +1648,6 @@
 
     upstream_part = own_quarter(cotangent.reshape(block, width))
     up_rows = dispatch(upstream_part)
-    upstream_part = upstream_part.astype(f32)
 
     flat_in = inputs.reshape(block, width).astype(f32)
     first_rms = inv_rms(flat_in)
@@ -1172,7 +1655,6 @@
     normed_own = (flat_in * first_rms).astype(bf16)
     own_gains = lax.dynamic_slice_in_dim(qk_gains, ctx * HEAD_DIM, HEAD_DIM, axis=1).astype(f32)
     own_gains = own_gains[:, None, :]
-    query_gain, key_gain = own_gains[0], own_gains[1]
     cosine, sine = signed_tables(0, length)
     (
         normed,
@@ -1186,23 +1668,10 @@
         attended,
         router_blocks,
     ) = attend(sizes, normed_own, qkv_scaled, own_gains, cosine, sine, router_own)
-    normed = normed.reshape(length, width)
     head_weight = head_weight.reshape(width, 3 * HEAD_DIM)
-    query_rms = qk_rms[:, :n_ctx].T.reshape(length, 1)
-    key_rms = qk_rms[:, n_ctx:].T.reshape(length, 1)
-    cosine, sine_table = rotary_tables(0, length)
-    scores = attend_scores(query_rot, key_rot, scale, block)
-    exponent = jnp.exp(scores - jnp.max(scores, axis=-1, keepdims=True))
-    probs = exponent / jnp.sum(exponent, axis=-1, keepdims=True)
-    probs_low = probs.astype(bf16)
     middle, small, chances, normed_mlp, rows, slot_gates = middle_stage(
         sizes, attended, out_all, in_part, router_blocks, pick.reshape(EXPERTS, CAP, block)
     )
-    second_rms = small[EXPERTS][:, None]
-    chances = chances.T
-    per = places // n_tp
-    router_part = lax.dynamic_slice_in_dim(router_blocks, tp * per, per, axis=0)
-    router_part = router_part.transpose(0, 2, 1).reshape(quarter, EXPERTS)
 
     back_rows, slot_products, act_low, pre_grads, returned = expert_stage(
         sizes, rows, up_rows.reshape(places, CAP, width), expert_weight, slot_gates
@@ -1210,7 +1679,6 @@
     rows = rows.reshape(EXPERTS * CAP, width)
     act_low = act_low.reshape(EXPERTS * CAP, hidden)
     pre_grads = pre_grads.reshape(EXPERTS * CAP, 2 * hidden)
-    back_part = combine(back_rows)
     output_part = (middle + bring_back(returned)).astype(bf16)
     rows_in = (((0,), (0,)), ((), ()))
     expert_grads = jnp.concatenate(
@@ -1223,89 +1691,67 @@
     expert_grads = lax.all_to_all(
         expert_grads.reshape(EXPERTS, depth, 3 * hidden), both, 0, 0, tiled=True
     ).astype(f32)
-    slot_products = lax.psum(slot_products[:, 0, :CAP], "tp")
-
-    chance_grads = jnp.sum(pick_f32 * slot_products[:, :, None], axis=1).T
-    logit_grads = chances * (chance_grads - jnp.sum(chances * chance_grads, axis=-1, keepdims=True))
-    scaled_mlp = back_part + jnp.dot(logit_grads, router_part.T, precision=highest)
-    inner = lax.psum(jnp.sum(scaled_mlp * middle, axis=-1, keepdims=True), "tp")
-    middle_grad = upstream_part + second_rms * scaled_mlp - middle * second_rms**3 / width * inner
+
+    middle_grad, branch_grad, logit_grads, proj_grads, gain_terms, inners = back_stage(
+        sizes,
+        back_rows,
+        pick_t,
+        pick.reshape(EXPERTS, CAP, block),
+        slot_products,
+        middle,
+        small,
+        chances,
+        upstream_part,
+        router_blocks,
+        out_all,
+        query_rot,
+        key_rot,
+        value_heads,
+        query_proj,
+        key_proj,
+        qk_rms,
+        own_gains,
+        cosine,
+        sine,
+    )
     router_term = lax.dot_general(
-        normed_mlp.astype(f32), logit_grads, rows_in, precision=highest
+        normed_mlp.astype(f32), logit_grads, (((0,), (1,)), ((), ())), precision=highest
     )
     router_term = lax.all_gather(router_term, "tp", axis=0, tiled=True)
     router_term = lax.psum_scatter(router_term, both, scatter_dimension=0, tiled=True)
     grad_router = router_term * mlp_scale[:, None]
-
-    branch_grad = lax.all_gather(middle_grad.astype(bf16), "tp", axis=1, tiled=True)
     grad_out = lax.dot_general(branch_grad, attended, rows_in, preferred_element_type=f32)
     grad_out = lax.psum_scatter(grad_out.astype(bf16), both, scatter_dimension=0, tiled=True)
-    attended_grad = jnp.dot(branch_grad, out_all, preferred_element_type=f32).astype(bf16)
-    attended_grad = attended_grad.reshape(block, n_ctx, HEAD_DIM).transpose(1, 0, 2)
-    attended_grad = lax.all_to_all(attended_grad, "ctx", 0, 0, tiled=True)
-    attended_grad = attended_grad.reshape(length, HEAD_DIM)
-    prob_grads = jnp.einsum(
-        "qd,kd->qk", attended_grad, value_heads, preferred_element_type=f32
-    )
-    score_grads = (
-        probs * (prob_grads - jnp.sum(probs * prob_grads, axis=-1, keepdims=True))
-    ).astype(bf16)
-    query_grads = jnp.dot(score_grads, key_rot, preferred_element_type=f32) * scale
-    key_grads = lax.dot_general(score_grads, query_rot, rows_in, preferred_element_type=f32) * scale
-    value_grads = lax.dot_general(probs_low, attended_grad, rows_in, preferred_element_type=f32)
-    query_norm_grad = rotate_back(query_grads, cosine, sine_table)
-    key_norm_grad = rotate_back(key_grads, cosine, sine_table)
-    query_scaled = query_norm_grad * query_gain
-    key_scaled = key_norm_grad * key_gain
-    inners = lax.psum(
-        jnp.stack([jnp.sum(query_scaled * query_proj, axis=-1), jnp.sum(key_scaled * key_proj, axis=-1)]),
-        ("ctx", "tp"),
-    )
-    query_pre = query_rms * query_scaled - query_proj * query_rms**3 / HQ * inners[0][:, None]
-    key_pre = key_rms * key_scaled - key_proj * key_rms**3 / HQ * inners[1][:, None]
-    gain_terms = jnp.stack(
-        [
-            jnp.sum(query_norm_grad * query_proj * query_rms, axis=0),
-            jnp.sum(key_norm_grad * key_proj * key_rms, axis=0),
-        ]
-    )
-    gain_terms = lax.all_gather(lax.psum(gain_terms, "fsdp"), "ctx", axis=1, tiled=True)
-    proj_grads = jnp.concatenate([query_pre, key_pre, value_grads], axis=1).astype(bf16)
-    qkv_grads = lax.dot_general(normed, proj_grads, rows_in, preferred_element_type=f32)
-    qkv_grads = lax.all_to_all(
-        qkv_grads.astype(bf16).reshape(places, depth, 3 * HEAD_DIM), both, 0, 0, tiled=True
-    )
-    qkv_grads = qkv_grads.astype(f32).reshape(n_fsdp, n_ctx, depth, 3 * HEAD_DIM).sum(axis=0)
+    gain_terms = lax.all_gather(
+        lax.psum(gain_terms.reshape(2, HEAD_DIM), "fsdp"), "ctx", axis=1, tiled=True
+    )
+    own_inners = lax.dynamic_index_in_dim(inners.reshape(block, 4, n_ctx), ctx, 2, keepdims=False)
+    own_rms = lax.dynamic_index_in_dim(qk_rms.reshape(block, 2, n_ctx), ctx, 2, keepdims=False)
+    first_inner = epsilon * jnp.sum(own_inners[:, :2] * own_rms**3, axis=1) + own_inners[:, 2]
+    columns = jnp.concatenate(
+        [first_rms, first_inner[:, None] * first_rms**2 / width], axis=1
+    )
+    grad_inputs, qkv_grads = final_stage(
+        sizes, proj_grads, head_weight, normed, in_part, middle_grad, columns
+    )
+    qkv_grads = qkv_grads.astype(f32)
     grad_qkv = (qkv_grads * attn_scale[None, :, None]).reshape(n_ctx, depth, 3, HEAD_DIM)
     grad_qkv = grad_qkv.transpose(1, 2, 0, 3).reshape(depth, 3, n_ctx * HEAD_DIM)
-    scaled_first = lax.dot_general(
-        proj_grads, head_weight, (((1,), (1,)), ((), ())), preferred_element_type=f32
-    ).astype(bf16)
-    scaled_first = lax.psum_scatter(scaled_first, "tp", scatter_dimension=1, tiled=True)
-    scaled_first = lax.psum_scatter(scaled_first, "ctx", scatter_dimension=0, tiled=True)
-    scaled_first = scaled_first.astype(f32)
     gains = jnp.stack(
         [
             jnp.sum(qkv_grads * qkv_raw, axis=(0, 2)),
             jnp.sum(expert_grads[:, :, : 2 * hidden] * gate_up_raw.astype(f32), axis=(0, 2)),
         ]
     )
-    last_inner = jnp.sum(scaled_first * in_part, axis=-1)
-    gains, last_inner = lax.psum((gains, last_inner), "tp")
+    gains = lax.psum(gains, "tp")
     grad_mlp_gain = gains[1] + jnp.sum(router_term * router_f32, axis=-1)
-    grad_inputs = (
-        middle_grad
-        + first_rms * scaled_first
-        - in_part * first_rms**3 / width * last_inner[:, None]
-    )
-    grad_inputs = lax.all_gather(grad_inputs.astype(bf16), "tp", axis=1, tiled=True).astype(f32)
     output = lax.all_gather(output_part, "tp", axis=1, tiled=True)
     grad_gate_up = (expert_grads[:, :, : 2 * hidden] * mlp_scale[None, :, None]).reshape(
         EXPERTS, depth, 2, hidden
     )
     return (
         output[None],
-        grad_inputs[None],
+        grad_inputs.astype(f32)[None],
         gains[0],
         grad_qkv,
         grad_out.astype(f32),

time: 779 us -> 657 us (0.84)
  waiting for transfers between devices: 230 us -> 29.6 us
  Pallas kernels: 269 us -> 427 us
  matrix products: 50.1 us -> 17.2 us
  blocking collectives: 69.2 us -> 46.7 us
  other arithmetic: 57.9 us -> 36.8 us
  starting transfers between devices: 30.2 us -> 21.6 us
    pallas_call x0 -> x2, Pallas kernels: none -> 157 us  [the longest x1 108 us: final_stage(): pl.pallas_call(functools.partial(final_kernel, sizes), name='final', out_...]
    all_to_all x1, waiting for transfers between devices: 73.5 us -> 0.01 us  [by_head(): lax.all_to_all(expert_grads.reshape(EXPERTS, depth, 3 * hidden), both, 0,...]
    psum x5 -> x2, blocking collectives: 53.6 us -> 10.6 us  [the longest x1 5.65 us: by_head(): gains = lax.psum(gains, 'tp')]
    reduce_scatter x1, waiting for transfers between devices: 36.3 us -> 4.42 us  [by_head(): lax.psum_scatter(grad_out.astype(bf16), both, scatter_dimension=0, tiled=...]
    all_to_all x2 -> x0, waiting for transfers between devices: 30.9 us -> none  [the longest x1 24.8 us: by_head(): lax.all_to_all(qkv_grads.astype(bf16).reshape(places, depth, 3 * HEAD_DIM...]
    dot_general x10 -> x1, matrix products: 30.1 us -> 0.9 us  [by_head(): lax.dot_general(normed_mlp.astype(f32), logit_grads, (((0,), (1,)), ((),...]
    all_gather x2 -> x0, waiting for transfers between devices: 27.9 us -> none  [the longest x1 14.5 us: by_head(): lax.all_gather(grad_inputs.astype(bf16), 'tp', axis=1, tiled=True)]
    reduce_scatter x1, waiting for transfers between devices: 27 us -> 0.01 us  [by_head(): lax.psum_scatter(router_term, both, scatter_dimension=0, tiled=True)]
  transfers between devices with their start and end apart: 16 -> 10, of which waited for: 10 -> 3; matrix products, arithmetic and copies ran while one was open for 16% -> 16% of each run, Pallas kernels for 28% -> 57%
where the time goes in v3:
time: 657 us; the launch traced here: 649 us
  Pallas kernels  427 us (65%)
  local copies, waits for them, and re-layouts  55.5 us (8%)
  blocking collectives  46.7 us (7%)
  other arithmetic  36.8 us (6%)
  waiting for transfers between devices  29.6 us (5%)
  starting transfers between devices  21.6 us (3%)
  matrix products  17.2 us (3%)
  between operations  14.8 us (2%)
    pallas_call x1, Pallas kernels, attend(): pl.pallas_call(functools.partial(attend_kernel, sizes, 1.0 / math.sqrt(HE...  150 us
    pallas_call x1, Pallas kernels, final_stage(): pl.pallas_call(functools.partial(final_kernel, sizes), name='final', out_...  108 us
    pallas_call x1, Pallas kernels, middle_stage(): pl.pallas_call(functools.partial(middle_kernel, sizes), name='middle', ou...  62.8 us
    pallas_call x1, Pallas kernels, expert_stage(): pl.pallas_call(functools.partial(expert_kernel, sizes), name='expert', ou...  56.5 us
    pallas_call x1, Pallas kernels, back_stage(): pl.pallas_call(functools.partial(back_kernel, sizes, 1.0 / math.sqrt(HEAD...  49.2 us
    all_gather x1, blocking collectives, by_head(): lax.all_gather(lax.psum(gain_terms.reshape(2, HEAD_DIM), 'fsdp'), 'ctx',...  30.5 us
    all_to_all x1, waiting for transfers between devices, bring_back(): return combine(lax.all_to_all(rows, both, 0, 0, tiled=True))  20.3 us
    unnamed x73, local copies, waits for them, and re-layouts  15.2 us
  transfers between devices with their start and end apart: 10, of which 3 were waited for; matrix products, arithmetic and copies ran while one was open for 16% of the time, Pallas kernels for 57%

profile of v3, /device:TPU:0, one launch (start us, length us, event | category | flops | bytes accessed | tf_op | source)
XLA Modules:
  0.0 649.1 jit_solution(16130332408949954498)
XLA Ops:
  10.6 1.6 convolution_convert_fusion.1
  12.2 7.2 %all-to-all-start = ((bf16[8,160,512]{2,1,0:T(8,128)(2,1)}), bf16[8,160,512]{2,1,0:T(8,128)(2,1)}, u32[]{:S(2)}, u32[]{:S(2)}) async-start(bf16[8,160,512]{2,1,0:T(8,128)(2,1)} %bitcast.11), calls=%async_computation | async-start | bytes 2621440 | tf_op jit(solution)/shard_map/all_to_all | solution.py:1635
  20.0 2.7 fusion.9
  22.9 2.6 convert_bitcast_fusion
  26.5 1.3 copy.83
  27.8 1.9 copy.84
  29.8 6.9 %copy.85 = f32[8,256,2,256]{3,2,1,0:T(2,128)} copy(f32[8,256,2,256]{3,0,2,1:T(8,128)} %convert_bitcast_fusion) | data formatting | bytes 8388608 | tf_op jit(solution)/shard_map/convert_element_type | solution.py:1614
  36.7 6.4 reshape.173
  43.1 2.5 copy.104
  45.6 1.2 fusion.18
  46.8 2.0 pad_maximum_fusion.3.sine
  49.1 2.9 multiply_convert_fusion
  52.1 2.0 pad_maximum_fusion
  56.9 3.4 all-to-all-done
  60.3 4.5 all-to-all-start.1
  65.8 150.5 %attend.1 = (bf16[4,256,2048]{2,1,0:T(8,128)(2,1)}, bf16[8,256,384]{2,1,0:T(8,128)(2,1)}, f32[1024,128]{1,0:T(8,128)}, f32[1024,128]{1,0:T(8,128)}, bf16[1024,12...) custom-call(bf16[256,2048]{1,0:T(8,128)(2,1)} %fusion.2.own_rows, ...), custom_call_target="tpu_custom_call" | custom-call | flops 70000001024 | bytes 20000000 | tf_op jit(solution)/shard_map/attend/pallas_call | solution.py:632
  217.4 62.8 %middle.1 = (f32[256,512]{1,0:T(8,128)}, f32[16,256]{1,0:T(8,128)}, f32[8,256]{1,0:T(8,128)}, bf16[256,512]{1,0:T(8,128)(2,1)}, bf16[8,160,2048]{2,1,0:T(8,128)(2,1)}, /*index=5*/f32[8,8,256]{2,1,0:T(8,128)}) custom-call(bf16[256,512]{1,0:T(8,128)(2,1)} %get-tuple-element.39.attended, bf16[2048,512]{1,0:T(8,128)(2,1)} %all-gather.4.cloned.1.call-done.out_all, ...), custom_call_target="tpu_custom_call" | custom-call | flops 60000002048 | bytes 20000000 | tf_op jit(solution)/shard_map/middle/pallas_call | solution.py:880
  280.2 56.5 %expert.1 = (bf16[8,160,512]{2,1,0:T(8,128)(2,1)}, f32[8,8,256]{2,1,0:T(8,128)}, bf16[8,160,256]{2,1,0:T(8,128)(2,1)}, bf16[8,160,512]{2,1,0:T(8,128)(2,1)}, bf16[8,160,2048]{2,1,0:T(8,128)(2,1)}) custom-call(bf16[8,160,2048]{2,1,0:T(8,128)(2,1)} %get-tuple-element.42.rows, bf16[8,160,2048]{2,1,0:T(8,128)(2,1)} %all-gather.6.cloned.1.call-done.up_rows, ...), custom_call_target="tpu_custom_call" | custom-call | flops 49999998976 | bytes 30000000 | tf_op jit(solution)/shard_map/expert/pallas_call | solution.py:1064
  338.5 1.7 copy.87
  341.4 49.2 %back.1 = (f32[256,512]{1,0:T(8,128)}, bf16[256,2048]{1,0:T(8,128)(2,1)}, f32[8,256]{1,0:T(8,128)}, bf16[1024,384]{1,0:T(8,128)(2,1)}, f32[2,1,128]{2,1,0:T(1,128)}, /*index=5*/f32[256,16]{1,0:T(8,128)}) custom-call(bf16[8,160,512]{2,1,0:T(8,128)(2,1)} %get-tuple-element.45.back, bf16[256,1280]{1,0:T(8,128)(2,1)} %compare_convert_fusion.pick_t, ...), custom_call_target="tpu_custom_call" | custom-call | flops 60000002048 | bytes 20000000 | tf_op jit(solution)/shard_map/back/pallas_call | solution.py:1331
  392.5 5.7 all_gather.19
  398.2 3.3 convolution_convert_fusion
  401.5 4.4 all-to-all-start.2
  407.3 4.2 fusion
  411.6 5.8 bitcast_convert_fusion
  417.4 1.8 pad_maximum_fusion.1
  419.2 20.3 %all-to-all-done.2 = bf16[8,160,512]{2,1,0:T(8,128)(2,1)S(1)} async-done(((bf16[8,160,512]{2,1,0:T(8,128)(2,1)}), bf16[8,160,512]{2,1,0:T(8,128)(2,1)S(1)}, u32[]{:S(2)}, u32[]{:S(2)}) %all-to-all-start.2) | async-done | bytes 1310752 | tf_op jit(solution)/shard_map/all_to_all | solution.py:1643
  440.6 4.5 all-to-all-start.3
  445.1 108.0 %final.1 = (bf16[256,2048]{1,0:T(8,128)(2,1)}, bf16[4,256,384]{2,1,0:T(8,128)(2,1)}) custom-call(bf16[1024,384]{1,0:T(8,128)(2,1)} %get-tuple-element.55.proj_grads, bf16[2048,384]{1,0:T(8,128)(2,1)} %bitcast.111, bf16[4,256,2048]{2,1,0:T(8,128)(2,1)} %get-tuple-element.57.normed, f32[256,512]{1,0:T(8,128)} %dynamic-slice_bitcast_fusion.in_part, ...), custom_call_target="tpu_custom_call" | custom-call | flops 60000002048 | bytes 20000000 | tf_op jit(solution)/shard_map/final/pallas_call | solution.py:1552
  553.1 2.9 bitcast_convert_fusion.1
  556.1 1.3 fusion.5
  557.8 1.5 convert_multiply_fusion
  559.3 1.9 copy.92
  561.2 1.4 copy.93
  562.6 3.1 copy.95
  565.6 4.9 psum.15
  570.6 30.5 %all_gather.18 = f32[2,512]{1,0:T(2,128)S(1)} all-gather(f32[2,128]{1,0:T(2,128)S(1)} %psum.15), channel_id=1, replica_groups=mesh['fsdp'=2,'ctx'=4,'tp'=4] {'ctx'}, dimensions={1}, use_global_device_ids=true | all-gather | bytes 5120 | tf_op jit(solution)/shard_map/all_gather | solution.py:1725
  601.1 1.3 broadcast_multiply_fusion.1
  602.4 4.4 reduce-scatter.6.cloned.1.call-done
  606.8 1.8 convert_element_type.123
  608.6 2.6 convert_element_type.121
  611.7 3.1 slice_multiply_fusion
  615.6 5.9 reshape.170
  621.5 6.7 %copy.103 = f32[8,256,2,256]{3,0,2,1:T(8,128)} copy(f32[8,256,2,256]{3,2,1,0:T(2,128)} %reshape.170) | data formatting | bytes 8388608 | tf_op jit(solution)/shard_map/reshape | solution.py:1749
  628.1 1.7 slice_bitcast_fusion
  629.9 2.5 copy.96
  632.4 5.6 psum.14
  639.2 2.3 copy.110
  (125 shorter events, 21.1 us)
Async XLA Ops:
  7.2 3.4 copy-start
  7.2 210.2 %all-gather.4.cloned.1.call-start = ((), (), s32[]{:S(2)}) async-start(), calls=%async_computation.7 | async-start | bytes 2359296 | tf_op jit(solution)/shard_map/all_gather | solution.py:1618
  8.8 0.6 copy-start.17
  10.6 1.6 copy-start.11
  10.6 8.9 %copy-start.13 = (bf16[256,3,512]{2,0,1:T(8,128)(2,1)S(1)}, bf16[256,3,512]{2,0,1:T(8,128)(2,1)}, u32[]{:S(2)}) copy-start(bf16[256,3,512]{2,0,1:T(8,128)(2,1)} %param.13) | copy-start | bytes 2359300
  12.2 48.1 %all-to-all-start = ((bf16[8,160,512]{2,1,0:T(8,128)(2,1)}), bf16[8,160,512]{2,1,0:T(8,128)(2,1)}, u32[]{:S(2)}, u32[]{:S(2)}) async-start(bf16[8,160,512]{2,1,0:T(8,128)(2,1)} %bitcast.11), calls=%async_computation | async-start | bytes 2621440 | tf_op jit(solution)/shard_map/all_to_all | solution.py:1635
  20.0 2.9 copy-start.8
  25.5 1.0 copy-start.28
  26.5 27.6 %copy-start.23 = (f32[256]{0:T(256)}, f32[256]{0:T(256)S(1)}, u32[]{:S(2)}) copy-start(f32[256]{0:T(256)S(1)} %convert_element_type.108) | copy-start | bytes 3076
  27.8 1.9 copy-start.29
  29.8 24.9 %copy-start.4 = (f32[4,256,384]{2,1,0:T(8,128)}, f32[4,256,384]{2,1,0:T(8,128)S(1)}, u32[]{:S(2)}) copy-start(f32[4,256,384]{2,1,0:T(8,128)S(1)} %copy.84) | copy-start | bytes 4718596
  29.8 24.9 %copy-start.25 = (f32[256]{0:T(256)}, f32[256]{0:T(256)S(1)}, u32[]{:S(2)}) copy-start(f32[256]{0:T(256)S(1)} %convert_element_type.104) | copy-start | bytes 3076
  43.1 5.8 copy-start.6
  49.1 2.9 copy-start.7
  52.1 2.0 copy-start.21
  54.1 1.7 copy-start.19
  60.3 219.8 %all-to-all-start.1 = ((bf16[8,256,768]{2,1,0:T(8,128)(2,1)}), bf16[8,256,768]{2,1,0:T(8,128)(2,1)}, u32[]{:S(2)}, u32[]{:S(2)}) async-start(bf16[8,256,768]{2,1,0:T(8,128)(2,1)} %pad_maximum_fusion), calls=%async_computation.1 | async-start | bytes 6291456 | tf_op jit(solution)/shard_map/all_to_all | solution.py:1616
  64.8 215.3 %all-gather.6.cloned.1.call-start = ((), (), s32[]{:S(2)}) async-start(), calls=%async_computation.8 | async-start | bytes 6553600 | tf_op jit(solution)/shard_map/all_gather | solution.py:1636
  65.6 336.0 %reduce-scatter.4.cloned.1.call-start = ((), (), s32[]{:S(2)}) async-start(), calls=%async_computation.9 | async-start | bytes 6553600 | tf_op jit(solution)/shard_map/reduce_scatter | solution.py:1640
  336.6 0.7 copy-start.18
  336.7 3.6 copy-start.16
  336.7 264.4 %reduce-scatter.8.cloned.1.call-start = ((), (), s32[]{:S(2)}) async-start(), calls=%async_computation.12 | async-start | bytes 73728 | tf_op jit(solution)/shard_map/reduce_scatter | solution.py:1721
  341.3 50.2 %copy-start.15 = (bf16[256,512]{1,0:T(8,128)(2,1)S(1)}, bf16[256,512]{1,0:T(8,128)(2,1)}, u32[]{:S(2)}) copy-start(bf16[256,512]{1,0:T(8,128)(2,1)} %get-tuple-element.66) | copy-start | bytes 786436
  341.4 56.8 %copy-start.14 = (bf16[256,512]{1,0:T(8,128)(2,1)S(1)}, bf16[256,512]{1,0:T(8,128)(2,1)}, u32[]{:S(2)}) copy-start(bf16[256,512]{1,0:T(8,128)(2,1)} %get-tuple-element.39.attended) | copy-start | bytes 786436
  401.4 5.0 copy-start.20
  401.5 5.8 copy-start.31
  401.5 38.0 %all-to-all-start.2 = ((bf16[8,160,512]{2,1,0:T(8,128)(2,1)}), bf16[8,160,512]{2,1,0:T(8,128)(2,1)S(1)}, u32[]{:S(2)}, u32[]{:S(2)}) async-start(bf16[8,160,512]{2,1,0:T(8,128)(2,1)} %reduce-scatter.4.cloned.1.call-done), calls=%async_computation.3 | async-start | bytes 2621440 | tf_op jit(solution)/shard_map/all_to_all | solution.py:1643
  406.0 200.8 %reduce-scatter.6.cloned.1.call-start = ((), (), s32[]{:S(2)}) async-start(), calls=%async_computation.11 | async-start | bytes 2359296 | tf_op jit(solution)/shard_map/reduce_scatter | solution.py:1724
  407.3 4.3 copy-start.32
  439.5 1.1 copy-start.9
  440.6 168.0 %all-to-all-start.3 = ((bf16[8,256,768]{2,1,0:T(8,128)(2,1)}), bf16[8,256,768]{2,1,0:T(8,128)(2,1)}, u32[]{:S(2)}, u32[]{:S(2)}) async-start(bf16[8,256,768]{2,1,0:T(8,128)(2,1)} %pad_maximum_fusion.1), calls=%async_computation.4 | async-start | bytes 6291456 | tf_op jit(solution)/shard_map/all_to_all | solution.py:1691
  445.0 194.2 %all-gather.8.cloned.1.call-start = ((), (), s32[]{:S(2)}) async-start(), calls=%async_computation.10 | async-start | bytes 1310720 | tf_op jit(solution)/shard_map/all_gather | solution.py:1748
  553.1 2.9 copy-start.10
  553.1 2.9 copy-start.30
  556.0 1.4 copy-start.5
  556.0 1.7 copy-start.12
  556.1 1.7 copy-start.26
  562.6 3.1 copy-start.27
  562.6 38.5 %copy-start.22 = (bf16[256,8]{0,1:T(8,128)(2,1)S(1)}, bf16[256,8]{0,1:T(8,128)(2,1)}, u32[]{:S(2)}) copy-start(bf16[256,8]{0,1:T(8,128)(2,1)} %param.17) | copy-start | bytes 12292
  562.6 38.5 %copy-start.24 = (f32[256]{0:T(256)S(1)}, f32[256]{0:T(256)}, u32[]{:S(2)}) copy-start(f32[256]{0:T(256)} %copy-done.23) | copy-start | bytes 3076
  608.6 3.1 copy-start.2
  611.7 3.9 copy-start.3
  629.9 12.2 %copy-start.1 = (bf16[1,256,2048]{2,1,0:T(8,128)(2,1)S(1)}, bf16[1,256,2048]{2,1,0:T(8,128)(2,1)}, u32[]{:S(2)}) copy-start(bf16[1,256,2048]{2,1,0:T(8,128)(2,1)} %param.21) | copy-start | bytes 3145732
Sparse Core Ops, SparseCore 0:
  10.2 87.1 all-gather.3
  98.9 63.8 all-gather.5
  336.8 58.8 reduce-scatter.3
  401.6 124.9 reduce-scatter.7
  530.9 75.8 reduce-scatter.5
  608.8 15.8 all-gather.7
